TPU v7x, 32 devices: a whole 2x2x4 slice. The times are simulated.
32 devices in a mesh: ctx: 8 (over y, x, core), fsdp: 4 (over z).
Axes of the slice: x: 2, y: 2, z: 4, core: 2. Of those that a mesh axis runs over, the one named last changes fastest.
Arguments:
- loaded: bfloat16 [8, 8, 128, 4096], P('ctx', None, None, 'fsdp'), may hold values from -6 to 6
- slot_pos: int32 [8, 8, 128], P('ctx'), may hold values from -1 to 255, as said below
- contig_lengths: int32 [16], replicated, may hold values from 1 to 1024, 2048 in all
- w_in: bfloat16 [4096, 3, 4096], P('ctx', None, 'fsdp'), may hold values from -0.09375 to 0.09375
- short_taps: float32 [3, 7, 4096], P(None, None, 'fsdp'), may hold values from -2 to 2
- long_taps: float32 [128, 4096], P(None, 'fsdp'), may hold values from -0.5 to 0.5
- grad_out: bfloat16 [2048, 4096], P('ctx', 'fsdp'), may hold values from -0.59765625 to 0.59765625
Outputs:
- gated_out: bfloat16 [2048, 4096], P('ctx', 'fsdp')
- token_grads: bfloat16 [2048, 4096], P('ctx', 'fsdp')
- weight_grads: bfloat16 [4096, 3, 4096], P('ctx', None, 'fsdp')
- short_grads: float32 [3, 7, 4096], P(None, None, 'fsdp')
- long_grads: float32 [128, 4096], P(None, 'fsdp')
Inputs may be any that keep to these rules, and one draw needn't show every extreme that they name: `slot_pos`: for each destination e, the slots with a value of 0 or more name every row 0 to 255 of e's block exactly once; -1 marks an empty slot; for each destination some loader fills all 128 of its slots. `contig_lengths`: the lengths sum to 2048.
All inputs are finite; a program needn't handle non-finite values.
Results may differ from a plain program's by a relative error of at most 0.012.
Values may be sent and summed in bfloat16 or wider, within the bound.
A program may use at most 192 MiB of HBM per device.

v0:
```python
import jax
import jax.numpy as jnp
from jax import lax
from jax.sharding import PartitionSpec as P


def passed_along(x, axis, by):
    size = lax.axis_size(axis)
    pairs = [(i, i + by) for i in range(size) if 0 <= i + by < size]
    return lax.ppermute(x, axis, pairs)


def starts_of(positions, contig_lengths):
    ends = jnp.cumsum(contig_lengths, dtype=jnp.int32)
    begins = ends - contig_lengths
    chosen = jnp.where(begins[None, :] <= positions[:, None], begins[None, :], 0)
    return jnp.max(chosen, axis=1)


def lead_filter(ext, taps, positions, begins_here):
    width = taps.shape[0]
    count = ext.shape[0] - width + 1
    bcast_shape = (count,) + (1,) * (ext.ndim - 1)
    total = jnp.zeros((count,) + ext.shape[1:], jnp.float32)
    for tap_index in range(width):
        keep_mask = (positions - tap_index >= begins_here).astype(jnp.float32).reshape(bcast_shape)
        first = width - 1 - tap_index
        total = total + taps[tap_index] * ext[first : first + count] * keep_mask
    return total


def trail_filter(ext, taps, positions, begins_ext):
    width = taps.shape[0]
    count = ext.shape[0] - width + 1
    bcast_shape = (count,) + (1,) * (ext.ndim - 1)
    total = jnp.zeros((count,) + ext.shape[1:], jnp.float32)
    for tap_index in range(width):
        keep_mask = (
            (positions >= begins_ext[tap_index : tap_index + count])
            .astype(jnp.float32)
            .reshape(bcast_shape)
        )
        total = total + taps[tap_index] * ext[tap_index : tap_index + count] * keep_mask
    return total


def tap_sums(grads, ext, width, lead_count, positions, begins_here):
    count = grads.shape[0]
    bcast_shape = (count,) + (1,) * (grads.ndim - 1)
    pieces = []
    for tap_index in range(width):
        keep_mask = (positions - tap_index >= begins_here).astype(jnp.float32).reshape(bcast_shape)
        first = lead_count - tap_index
        pieces.append(jnp.sum(grads * ext[first : first + count] * keep_mask, axis=0))
    return jnp.stack(pieces, 0)


def on_device(loaded, slot_pos, contig_lengths, w_in, short_taps, long_taps, grad_out):
    moved = lax.all_to_all(loaded, "ctx", split_axis=1, concat_axis=0, tiled=True)
    feat_cols = moved.shape[3]
    slot_rows = moved.reshape(-1, feat_cols)
    tok_rows = grad_out.shape[0]
    short_width = short_taps.shape[1]
    long_width = long_taps.shape[0]
    targets = slot_pos.reshape(-1)
    picker = (targets[None, :] == jnp.arange(tok_rows, dtype=jnp.int32)[:, None]).astype(
        jnp.bfloat16
    )
    own_part = jnp.dot(picker, slot_rows, preferred_element_type=jnp.float32).astype(jnp.bfloat16)
    tokens = lax.all_gather(own_part, "fsdp", axis=1, tiled=True)
    gathered = lax.all_gather(w_in, "ctx", axis=0, tiled=True)
    streams = jnp.einsum("td,dsc->tsc", tokens, gathered, preferred_element_type=jnp.float32)
    proj_half = streams.astype(jnp.bfloat16)
    offset = lax.axis_index("ctx") * tok_rows
    positions = offset + jnp.arange(tok_rows, dtype=jnp.int32)
    begins_here = starts_of(positions, contig_lengths)
    short_lags = jnp.transpose(short_taps, (1, 0, 2))
    prev_rows = passed_along(proj_half[tok_rows - (short_width - 1) :], "ctx", 1)
    lead_mixed = jnp.concatenate([prev_rows, proj_half], 0).astype(jnp.float32)
    lead_count = short_width - 1
    filtered = lead_filter(lead_mixed, short_lags, positions, begins_here)
    product = (filtered[:, 1] * filtered[:, 2]).astype(jnp.bfloat16)
    prior_rows = passed_along(product[tok_rows - (long_width - 1) :], "ctx", 1)
    lead_product = jnp.concatenate([prior_rows, product], 0).astype(jnp.float32)
    carried = lead_filter(lead_product, long_taps, positions, begins_here)
    gated_out = (filtered[:, 0] * carried).astype(jnp.bfloat16)
    upstream = grad_out.astype(jnp.float32)
    back_prod = (upstream * filtered[:, 0]).astype(jnp.bfloat16)
    first_grad = upstream * carried
    next_rows = passed_along(back_prod[: long_width - 1], "ctx", -1)
    long_begins = starts_of(
        offset + jnp.arange(tok_rows + long_width - 1, dtype=jnp.int32), contig_lengths
    )
    trail_prod = jnp.concatenate([back_prod, next_rows], 0).astype(jnp.float32)
    grad_product = trail_filter(trail_prod, long_taps, positions, long_begins)
    grad_filtered = jnp.stack(
        [first_grad, grad_product * filtered[:, 2], grad_product * filtered[:, 1]], 1
    ).astype(jnp.bfloat16)
    next_grads = passed_along(grad_filtered[: short_width - 1], "ctx", -1)
    short_begins = starts_of(
        offset + jnp.arange(tok_rows + short_width - 1, dtype=jnp.int32), contig_lengths
    )
    trail_grad = jnp.concatenate([grad_filtered, next_grads], 0).astype(jnp.float32)
    grad_mixed = trail_filter(trail_grad, short_lags, positions, short_begins).astype(jnp.bfloat16)
    long_local = tap_sums(
        back_prod.astype(jnp.float32),
        lead_product,
        long_width,
        long_width - 1,
        positions,
        begins_here,
    )
    short_local = tap_sums(
        grad_filtered.astype(jnp.float32),
        lead_mixed,
        short_width,
        lead_count,
        positions,
        begins_here,
    )
    short_total, long_total = (
        lax.psum(jnp.transpose(short_local, (1, 0, 2)).astype(jnp.bfloat16), "ctx").astype(
            jnp.float32
        ),
        lax.psum(long_local.astype(jnp.bfloat16), "ctx").astype(jnp.float32),
    )
    partial_value = jnp.einsum(
        "tsc,dsc->td", grad_mixed, gathered, preferred_element_type=jnp.float32
    )
    token_grads = lax.psum_scatter(
        partial_value.astype(jnp.bfloat16), "fsdp", scatter_dimension=1, tiled=True
    )
    weight_grads = lax.psum_scatter(
        jnp.einsum("td,tsc->dsc", tokens, grad_mixed, preferred_element_type=jnp.float32).astype(
            jnp.bfloat16
        ),
        "ctx",
        scatter_dimension=0,
        tiled=True,
    )
    return (gated_out, token_grads, weight_grads, short_total, long_total)


def solution(mesh):
    in_specs = (
        P("ctx", None, None, "fsdp"),
        P("ctx", None, None),
        P(),
        P("ctx", None, "fsdp"),
        P(None, None, "fsdp"),
        P(None, "fsdp"),
        P("ctx", "fsdp"),
    )
    out_specs = (
        P("ctx", "fsdp"),
        P("ctx", "fsdp"),
        P("ctx", None, "fsdp"),
        P(None, None, "fsdp"),
        P(None, "fsdp"),
    )
    return jax.shard_map(
        on_device, mesh=mesh, in_specs=in_specs, out_specs=out_specs, check_vma=False
    )
```

profile of v0, /device:TPU:15, one launch (start us, length us, event | category | flops | bytes accessed | tf_op | source)
XLA Modules:
  0.0 700.1 jit_solution(11985297371757299991)
XLA Ops:
  7.2 28.4 %all_to_all.4 = bf16[1,8,128,1024]{3,2,0,1:T(8,128)(2,1)S(1)} all-to-all(bf16[1,8,128,1024]{3,2,0,1:T(8,128)(2,1)} %bitcast.209), channel_id=1, replica_groups=mesh['ctx'=8,'fsdp'=4] {'ctx'}, dimensions={1} | all-to-all | bytes 4194304 | tf_op jit(solution)/shard_map/all_to_all | solution.py:59
  35.6 1.5 convolution_convert_fusion.1
  37.2 0.7 all-gather.5.cloned.1.call-update
  38.5 0.7 compare_convert_fusion.102
  39.3 0.7 compare_convert_fusion.129
  40.0 0.7 compare_convert_fusion.130
  40.7 0.7 compare_convert_fusion.131
  41.5 0.7 compare_convert_fusion.132
  42.2 0.7 compare_convert_fusion.133
  42.9 0.7 compare_convert_fusion.134
  45.1 0.7 fusion.558
  46.5 0.7 fusion.556
  47.2 0.7 fusion.555
  47.9 1.4 compare_convert_fusion.219
  49.7 32.9 %all-gather.3.cloned.1.call-done = bf16[256,4096]{1,0:T(8,128)(2,1)} async-done(((bf16[256,1024]{1,0:T(8,128)(2,1)}), bf16[256,4096]{1,0:T(8,128)(2,1)}) %all-gather.3.cloned.1.call-update) | async-done | bytes 2097168 | tf_op jit(solution)/shard_map/all_gather | solution.py:70
  82.6 127.3 %all-gather.5.cloned.1.call-done = bf16[4096,3,1024]{2,0,1:T(8,128)(2,1)} async-done(((bf16[512,3,1024]{2,0,1:T(8,128)(2,1)}), bf16[4096,3,1024]{2,0,1:T(8,128)(2,1)}) %all-gather.5.cloned.1.call-update) | async-done | bytes 25165840 | tf_op jit(solution)/shard_map/all_gather | solution.py:71
  209.9 12.2 %fusion.32 = bf16[256,3,1024]{2,0,1:T(8,128)(2,1)S(1)} fusion(bf16[4096,3,1024]{2,0,1:T(8,128)(2,1)} %all-gather.5.cloned.1.call-done, bf16[256,4096]{1,0:T(8,128)(2,1)} %all-gather.3.cloned.1.call-done), kind=kOutput, calls=%fused_computation.177 | convolution fusion | flops 6443237376 | bytes 28835840 | tf_op jit(solution)/shard_map/td,dsc->tsc/dot_general | solution.py:72
  222.1 1.3 collective-permute-start
  224.1 1.1 collective-permute-done
  225.8 3.6 multiply_add_fusion
  229.7 1.4 collective-permute-start.1
  232.5 2.8 collective-permute-done.1
  235.5 3.4 fusion.266
  238.9 0.8 slice.2608
  239.7 7.1 %collective-permute-start.2 = (bf16[127,1024]{1,0:T(8,128)(2,1)}, bf16[127,1024]{1,0:T(8,128)(2,1)S(1)}, u32[]{:S(2)}, u32[]{:S(2)}) collective-permute-start(bf16[127,1024]{1,0:T(8,128)(2,1)} %slice.2608), channel_id=1, source_target_pairs={{4,0},{8,4},{12,8},{16,12},{20,16},{24,20},{28,24},{5,1},{9,5},{13... | collective-permute-start | bytes 780296 | tf_op jit(solution)/shard_map/ppermute | solution.py:10
  246.8 3.3 fusion.268
  250.1 3.3 fusion.270
  253.4 3.3 fusion.272
  256.7 3.3 fusion.274
  260.0 3.1 fusion.276
  263.1 3.3 fusion.278
  266.4 3.3 fusion.280
  269.7 3.3 fusion.282
  273.0 3.3 fusion.284
  276.3 3.3 fusion.286
  279.7 3.4 fusion.288
  283.5 3.3 fusion.290
  287.2 9.1 %multiply_add_fusion.2 = f32[256,1024]{1,0:T(8,128)S(1)} fusion(f32[383,1024]{1,0:T(8,128)S(1)} %maximum_convert_fusion.2, f32[256]{0:T(256)} %copy-done.108, f32[1024]{0:T(1024)S(1)} %bitcast.309, f32[256]{0:T(256)} %copy-done.109, f32[1024]{0:T(1024)S(1)} %bitcast.312, f32[256]{0:T(256)} %copy-done.110, f32[1024]{0:T(1024)S(1)} %bitcast.314, ...), kind=kLoop, calls=%fused_computation.832 | loop fusion | flops 33554432 | bytes 46357504 | tf_op jit(solution)/shard_map/add | solution.py:28
  296.3 19.1 %fusion.550 = (bf16[256,1,1024]{2,0,1:T(8,128)(2,1)}, f32[256,1024]{1,0:T(8,128)}) fusion(bf16[256,1024]{1,0:T(8,128)(2,1)} %param.13, f32[256]{0:T(256)} %get-tuple-element.435, f32[383,1024]{1,0:T(8,128)S(1)} %maximum_convert_fusion.2, f32[1024]{0:T(1024)} %bitcast.279, f32[256]{0:T(256)} %get-tuple-element.436, f32[1024]{0:T(1024)} %bitcast.281, ...), kind=kLoop, calls=%fused_computation.840 | loop fusion | flops 67633152 | bytes 92709888 | tf_op jit(solution)/shard_map/stack | solution.py:96
  315.6 3.2 fusion.292
  318.8 1.2 maximum_convert_fusion.3
  320.4 8.2 %fusion.486 = f32[256,1024]{1,0:T(8,128)} fusion(f32[383,1024]{1,0:T(8,128)S(1)} %maximum_convert_fusion.3, f32[256]{0:T(256)} %get-tuple-element.407, f32[256]{0:T(256)} %get-tuple-element.408, f32[256]{0:T(256)} %get-tuple-element.409, f32[256]{0:T(256)} %get-tuple-element.410, f32[256]{0:T(256)} %get-tuple-element.411, f32[256]{0:T(256)} %get-tuple-element.412, ...), kind=kLoop, calls=%fused_computation.732 | loop fusion | flops 24903680 | bytes 34766848 | tf_op jit(solution)/shard_map/add | solution.py:43
  328.8 25.0 %fusion.548 = (bf16[256,1,1024]{2,0,1:T(8,128)(2,1)}, f32[256,1024]{1,0:T(8,128)}) fusion(f32[256,3,1024]{2,0,1:T(8,128)} %copy-done.4, f32[256]{0:T(256)} %get-tuple-element.307, f32[383,1024]{1,0:T(8,128)S(1)} %maximum_convert_fusion.3, f32[1024]{0:T(1024)S(1)} %bitcast.280, f32[256]{0:T(256)} %get-tuple-element.308, f32[1024]{0:T(1024)S(1)} %bitcast.282, ...), kind=kLoop, calls=%fused_computation.838 | loop fusion | flops 76021760 | bytes 104824832 | tf_op jit(solution)/shard_map/stack | solution.py:96
  353.9 3.4 fusion.549
  357.8 1.9 collective-permute-start.3
  360.9 0.7 stack.681
  368.2 0.7 stack.675
  375.6 0.7 stack.669
  386.9 0.7 stack.652
  388.3 0.7 stack.654
  392.3 0.7 stack.643
  401.6 0.7 stack.640
  413.1 0.7 stack.623
  420.6 10.6 %stack.704 = bf16[128,1024]{1,0:T(8,128)(2,1)} concatenate(bf16[1,1024]{1,0:T(2,128)(2,1)S(1)} %stack.576, bf16[1,1024]{1,0:T(2,128)(2,1)S(1)} %stack.577, bf16[1,1024]{1,0:T(2,128)(2,1)S(1)} %stack.578, bf16[1,1024]{1,0:T(2,128)(2,1)S(1)} %stack.579, bf16[1,1024]{1,0:T(2,128)(2,1)S(1)} %stack.580, bf16[1,1024]{1,0:T(2,128)(2,1)S(1)} %stack.581, bf16[1,1024]{1,0:T(2,128)(2,1)S(1)} %stack.582, ...), dimensions={0} | concatenate | bytes 524288 | tf_op jit(solution)/shard_map/stack | solution.py:55
  431.8 3.9 fusion.17
  435.7 13.3 %fusion = bf16[256,4096]{1,0:T(8,128)(2,1)} fusion(bf16[256,3,1024]{2,0,1:T(8,128)(2,1)S(1)} %fusion.17, bf16[4096,3,1024]{2,0,1:T(8,128)(2,1)} %all-gather.5.cloned.1.call-done), kind=kOutput, calls=%fused_computation.137 | convolution fusion | flops 6443499520 | bytes 28835840 | tf_op jit(solution)/shard_map/tsc,dsc->td/dot_general | solution.py:127
  449.1 13.4 %convolution_convert_fusion = bf16[4096,3,1024]{2,0,1:T(8,128)(2,1)} fusion(bf16[256,3,1024]{2,0,1:T(8,128)(2,1)S(1)} %fusion.17, bf16[256,4096]{1,0:T(8,128)(2,1)} %all-gather.3.cloned.1.call-done), kind=kOutput, calls=%fused_computation.128 | convolution fusion | flops 6455033856 | bytes 28835840 | tf_op jit(solution)/shard_map/td,tsc->dsc/dot_general | solution.py:134
  462.6 22.7 %all-reduce.2.cloned.1.call-done = bf16[128,1024]{1,0:T(8,128)(2,1)} async-done(((bf16[128,1024]{1,0:T(8,128)(2,1)}), bf16[128,1024]{1,0:T(8,128)(2,1)}) %all-reduce.2.cloned.1.call-update) | async-done | bytes 262160 | tf_op jit(solution)/shard_map/psum | solution.py:125
  485.3 1.9 convert_element_type.1809
  487.2 2.1 fusion.2
  489.4 3.7 fusion.14
  493.2 23.5 %psum.14 = bf16[3,7,1024]{2,0,1:T(4,128)(2,1)S(1)} all-reduce(bf16[3,7,1024]{2,0,1:T(4,128)(2,1)S(1)} %bitcast.214), channel_id=1, replica_groups=mesh['ctx'=8,'fsdp'=4] {'ctx'}, use_global_device_ids=true, to_apply=%region_13.14 | all-reduce | flops 21504 | bytes 86016 | tf_op jit(solution)/shard_map/psum | solution.py:122
  517.4 14.0 %reduce-scatter.3.cloned.1.call-done = bf16[256,1024]{1,0:T(8,128)(2,1)} async-done(((bf16[256,4096]{1,0:T(8,128)(2,1)}), bf16[256,1024]{1,0:T(8,128)(2,1)}) %reduce-scatter.3.cloned.1.call-update) | async-done | bytes 524304 | tf_op jit(solution)/shard_map/reduce_scatter | solution.py:130
  531.4 161.7 %reduce-scatter.5.cloned.1.call-done = bf16[512,3,1024]{2,0,1:T(8,128)(2,1)} async-done(((bf16[4096,3,1024]{2,0,1:T(8,128)(2,1)}), bf16[512,3,1024]{2,0,1:T(8,128)(2,1)}) %reduce-scatter.5.cloned.1.call-update) | async-done | bytes 3145744 | tf_op jit(solution)/shard_map/reduce_scatter | solution.py:133
  (539 shorter events, 62.4 us)
Async XLA Ops:
  7.2 75.4 %all-gather.3.cloned.1.call-start = ((), (), s32[]{:S(2)}) async-start(), calls=%async_computation.3 | async-start | bytes 2621440 | tf_op jit(solution)/shard_map/all_gather | solution.py:70
  37.2 172.7 %all-gather.5.cloned.1.call-start = ((), (), s32[]{:S(2)}) async-start(), calls=%async_computation.4 | async-start | bytes 28311552 | tf_op jit(solution)/shard_map/all_gather | solution.py:71
  37.9 447.3 %all-reduce.2.cloned.1.call-start = ((), (), s32[]{:S(2)}) async-start(), calls=%async_computation.7 | async-start | bytes 524288 | tf_op jit(solution)/shard_map/psum | solution.py:125
  49.3 176.5 %copy-start.89 = (f32[256]{0:T(256)}, f32[256]{0:T(256)S(1)}, u32[]{:S(2)}) copy-start(f32[256]{0:T(256)S(1)} %get-tuple-element.555) | copy-start | bytes 3076
  49.3 176.5 %copy-start.92 = (f32[256]{0:T(256)}, f32[256]{0:T(256)S(1)}, u32[]{:S(2)}) copy-start(f32[256]{0:T(256)S(1)} %get-tuple-element.556) | copy-start | bytes 3076
  49.3 176.5 %copy-start.95 = (f32[256]{0:T(256)}, f32[256]{0:T(256)S(1)}, u32[]{:S(2)}) copy-start(f32[256]{0:T(256)S(1)} %get-tuple-element.557) | copy-start | bytes 3076
  49.3 176.5 %copy-start.98 = (f32[256]{0:T(256)}, f32[256]{0:T(256)S(1)}, u32[]{:S(2)}) copy-start(f32[256]{0:T(256)S(1)} %get-tuple-element.558) | copy-start | bytes 3076
  49.3 176.5 %copy-start.101 = (f32[256]{0:T(256)}, f32[256]{0:T(256)S(1)}, u32[]{:S(2)}) copy-start(f32[256]{0:T(256)S(1)} %get-tuple-element.559) | copy-start | bytes 3076
  49.3 176.5 %copy-start.104 = (f32[256]{0:T(256)}, f32[256]{0:T(256)S(1)}, u32[]{:S(2)}) copy-start(f32[256]{0:T(256)S(1)} %get-tuple-element.560) | copy-start | bytes 3076
  49.3 176.5 %copy-start.106 = (f32[256]{0:T(256)}, f32[256]{0:T(256)S(1)}, u32[]{:S(2)}) copy-start(f32[256]{0:T(256)S(1)} %get-tuple-element.561) | copy-start | bytes 3076
  49.4 186.1 %copy-start.138 = (f32[256]{0:T(256)}, f32[256]{0:T(256)S(1)}, u32[]{:S(2)}) copy-start(f32[256]{0:T(256)S(1)} %get-tuple-element.448) | copy-start | bytes 3076
  49.4 220.3 %copy-start.108 = (f32[256]{0:T(256)}, f32[256]{0:T(256)S(1)}, u32[]{:S(2)}) copy-start(f32[256]{0:T(256)S(1)} %get-tuple-element.519) | copy-start | bytes 3076
  49.4 220.3 %copy-start.109 = (f32[256]{0:T(256)}, f32[256]{0:T(256)S(1)}, u32[]{:S(2)}) copy-start(f32[256]{0:T(256)S(1)} %get-tuple-element.520) | copy-start | bytes 3076
  49.4 223.6 %copy-start.110 = (f32[256]{0:T(256)}, f32[256]{0:T(256)S(1)}, u32[]{:S(2)}) copy-start(f32[256]{0:T(256)S(1)} %get-tuple-element.521) | copy-start | bytes 3076
  49.4 223.5 %copy-start.111 = (f32[256]{0:T(256)}, f32[256]{0:T(256)S(1)}, u32[]{:S(2)}) copy-start(f32[256]{0:T(256)S(1)} %get-tuple-element.522) | copy-start | bytes 3076
  49.4 223.5 %copy-start.112 = (f32[256]{0:T(256)}, f32[256]{0:T(256)S(1)}, u32[]{:S(2)}) copy-start(f32[256]{0:T(256)S(1)} %get-tuple-element.523) | copy-start | bytes 3076
  49.4 223.5 %copy-start.113 = (f32[256]{0:T(256)}, f32[256]{0:T(256)S(1)}, u32[]{:S(2)}) copy-start(f32[256]{0:T(256)S(1)} %get-tuple-element.524) | copy-start | bytes 3076
  49.4 223.5 %copy-start.114 = (f32[256]{0:T(256)}, f32[256]{0:T(256)S(1)}, u32[]{:S(2)}) copy-start(f32[256]{0:T(256)S(1)} %get-tuple-element.525) | copy-start | bytes 3076
  49.4 223.5 %copy-start.115 = (f32[256]{0:T(256)}, f32[256]{0:T(256)S(1)}, u32[]{:S(2)}) copy-start(f32[256]{0:T(256)S(1)} %get-tuple-element.526) | copy-start | bytes 3076
  49.4 223.5 %copy-start.116 = (f32[256]{0:T(256)}, f32[256]{0:T(256)S(1)}, u32[]{:S(2)}) copy-start(f32[256]{0:T(256)S(1)} %get-tuple-element.527) | copy-start | bytes 3076
  49.5 223.5 %copy-start.117 = (f32[256]{0:T(256)}, f32[256]{0:T(256)S(1)}, u32[]{:S(2)}) copy-start(f32[256]{0:T(256)S(1)} %get-tuple-element.528) | copy-start | bytes 3076
  49.5 226.8 %copy-start.118 = (f32[256]{0:T(256)}, f32[256]{0:T(256)S(1)}, u32[]{:S(2)}) copy-start(f32[256]{0:T(256)S(1)} %get-tuple-element.529) | copy-start | bytes 3076
  49.5 226.8 %copy-start.119 = (f32[256]{0:T(256)}, f32[256]{0:T(256)S(1)}, u32[]{:S(2)}) copy-start(f32[256]{0:T(256)S(1)} %get-tuple-element.530) | copy-start | bytes 3076
  49.5 226.8 %copy-start.120 = (f32[256]{0:T(256)}, f32[256]{0:T(256)S(1)}, u32[]{:S(2)}) copy-start(f32[256]{0:T(256)S(1)} %get-tuple-element.531) | copy-start | bytes 3076
  49.5 226.8 %copy-start.121 = (f32[256]{0:T(256)}, f32[256]{0:T(256)S(1)}, u32[]{:S(2)}) copy-start(f32[256]{0:T(256)S(1)} %get-tuple-element.532) | copy-start | bytes 3076
  49.5 226.8 %copy-start.122 = (f32[256]{0:T(256)}, f32[256]{0:T(256)S(1)}, u32[]{:S(2)}) copy-start(f32[256]{0:T(256)S(1)} %get-tuple-element.533) | copy-start | bytes 3076
  49.5 226.8 %copy-start.123 = (f32[256]{0:T(256)}, f32[256]{0:T(256)S(1)}, u32[]{:S(2)}) copy-start(f32[256]{0:T(256)S(1)} %get-tuple-element.534) | copy-start | bytes 3076
  49.5 226.8 %copy-start.124 = (f32[256]{0:T(256)}, f32[256]{0:T(256)S(1)}, u32[]{:S(2)}) copy-start(f32[256]{0:T(256)S(1)} %get-tuple-element.535) | copy-start | bytes 3076
  49.5 226.8 %copy-start.125 = (f32[256]{0:T(256)}, f32[256]{0:T(256)S(1)}, u32[]{:S(2)}) copy-start(f32[256]{0:T(256)S(1)} %get-tuple-element.536) | copy-start | bytes 3076
  49.5 230.1 %copy-start.126 = (f32[256]{0:T(256)}, f32[256]{0:T(256)S(1)}, u32[]{:S(2)}) copy-start(f32[256]{0:T(256)S(1)} %get-tuple-element.537) | copy-start | bytes 3076
  49.6 230.1 %copy-start.127 = (f32[256]{0:T(256)}, f32[256]{0:T(256)S(1)}, u32[]{:S(2)}) copy-start(f32[256]{0:T(256)S(1)} %get-tuple-element.538) | copy-start | bytes 3076
  49.6 230.1 %copy-start.128 = (f32[256]{0:T(256)}, f32[256]{0:T(256)S(1)}, u32[]{:S(2)}) copy-start(f32[256]{0:T(256)S(1)} %get-tuple-element.539) | copy-start | bytes 3076
  49.6 230.1 %copy-start.129 = (f32[256]{0:T(256)}, f32[256]{0:T(256)S(1)}, u32[]{:S(2)}) copy-start(f32[256]{0:T(256)S(1)} %get-tuple-element.540) | copy-start | bytes 3076
  49.6 230.1 %copy-start.130 = (f32[256]{0:T(256)}, f32[256]{0:T(256)S(1)}, u32[]{:S(2)}) copy-start(f32[256]{0:T(256)S(1)} %get-tuple-element.541) | copy-start | bytes 3076
  49.6 230.1 %copy-start.131 = (f32[256]{0:T(256)}, f32[256]{0:T(256)S(1)}, u32[]{:S(2)}) copy-start(f32[256]{0:T(256)S(1)} %get-tuple-element.542) | copy-start | bytes 3076
  49.6 230.1 %copy-start.132 = (f32[256]{0:T(256)}, f32[256]{0:T(256)S(1)}, u32[]{:S(2)}) copy-start(f32[256]{0:T(256)S(1)} %get-tuple-element.543) | copy-start | bytes 3076
  49.6 230.1 %copy-start.133 = (f32[256]{0:T(256)}, f32[256]{0:T(256)S(1)}, u32[]{:S(2)}) copy-start(f32[256]{0:T(256)S(1)} %get-tuple-element.544) | copy-start | bytes 3076
  49.6 233.5 %copy-start.134 = (f32[256]{0:T(256)}, f32[256]{0:T(256)S(1)}, u32[]{:S(2)}) copy-start(f32[256]{0:T(256)S(1)} %get-tuple-element.545) | copy-start | bytes 3076
  49.6 233.5 %copy-start.135 = (f32[256]{0:T(256)}, f32[256]{0:T(256)S(1)}, u32[]{:S(2)}) copy-start(f32[256]{0:T(256)S(1)} %get-tuple-element.546) | copy-start | bytes 3076
  49.6 233.5 %copy-start.136 = (f32[256]{0:T(256)}, f32[256]{0:T(256)S(1)}, u32[]{:S(2)}) copy-start(f32[256]{0:T(256)S(1)} %get-tuple-element.547) | copy-start | bytes 3076
  222.1 3.1 collective-permute-start
  229.7 5.6 collective-permute-start.1
  238.9 76.4 %copy-start.2 = (bf16[256,1024]{1,0:T(8,128)(2,1)}, bf16[256,1024]{1,0:T(8,128)(2,1)S(1)}, u32[]{:S(2)}) copy-start(bf16[256,1024]{1,0:T(8,128)(2,1)S(1)} %get-tuple-element.154) | copy-start | bytes 1572868
  239.7 79.1 %collective-permute-start.2 = (bf16[127,1024]{1,0:T(8,128)(2,1)}, bf16[127,1024]{1,0:T(8,128)(2,1)S(1)}, u32[]{:S(2)}, u32[]{:S(2)}) collective-permute-start(bf16[127,1024]{1,0:T(8,128)(2,1)} %slice.2608), channel_id=1, source_target_pairs={{4,0},{8,4},{12,8},{16,12},{20,16},{24,20},{28,24},{5,1},{9,5},{13... | collective-permute-start | bytes 780296 | tf_op jit(solution)/shard_map/ppermute | solution.py:10
  357.3 74.0 %copy-start.9 = (bf16[256,1,1024]{2,0,1:T(8,128)(2,1)}, bf16[256,1,1024]{2,0,1:T(8,128)(2,1)S(1)}, u32[]{:S(2)}) copy-start(bf16[256,1,1024]{2,0,1:T(8,128)(2,1)S(1)} %get-tuple-element.162) | copy-start | bytes 1572868
  357.5 56.8 %copy-start.154 = (bf16[1024]{0:T(1024)(128)(2,1)S(1)}, bf16[1024]{0:T(1024)(128)(2,1)}, u32[]{:S(2)}) copy-start(bf16[1024]{0:T(1024)(128)(2,1)} %get-tuple-element.46) | copy-start | bytes 6148
  357.5 56.9 %copy-start.153 = (bf16[1024]{0:T(1024)(128)(2,1)S(1)}, bf16[1024]{0:T(1024)(128)(2,1)}, u32[]{:S(2)}) copy-start(bf16[1024]{0:T(1024)(128)(2,1)} %get-tuple-element.47) | copy-start | bytes 6148
  357.5 56.9 %copy-start.152 = (bf16[1024]{0:T(1024)(128)(2,1)S(1)}, bf16[1024]{0:T(1024)(128)(2,1)}, u32[]{:S(2)}) copy-start(bf16[1024]{0:T(1024)(128)(2,1)} %get-tuple-element.48) | copy-start | bytes 6148
  357.5 56.9 %copy-start.151 = (bf16[1024]{0:T(1024)(128)(2,1)S(1)}, bf16[1024]{0:T(1024)(128)(2,1)}, u32[]{:S(2)}) copy-start(bf16[1024]{0:T(1024)(128)(2,1)} %get-tuple-element.49) | copy-start | bytes 6148
  357.5 56.9 %copy-start.150 = (bf16[1024]{0:T(1024)(128)(2,1)S(1)}, bf16[1024]{0:T(1024)(128)(2,1)}, u32[]{:S(2)}) copy-start(bf16[1024]{0:T(1024)(128)(2,1)} %get-tuple-element.50) | copy-start | bytes 6148
  357.5 56.9 %copy-start.149 = (bf16[1024]{0:T(1024)(128)(2,1)S(1)}, bf16[1024]{0:T(1024)(128)(2,1)}, u32[]{:S(2)}) copy-start(bf16[1024]{0:T(1024)(128)(2,1)} %get-tuple-element.51) | copy-start | bytes 6148
  357.5 56.9 %copy-start.148 = (bf16[1024]{0:T(1024)(128)(2,1)S(1)}, bf16[1024]{0:T(1024)(128)(2,1)}, u32[]{:S(2)}) copy-start(bf16[1024]{0:T(1024)(128)(2,1)} %get-tuple-element.52) | copy-start | bytes 6148
  357.5 56.9 %copy-start.147 = (bf16[1024]{0:T(1024)(128)(2,1)S(1)}, bf16[1024]{0:T(1024)(128)(2,1)}, u32[]{:S(2)}) copy-start(bf16[1024]{0:T(1024)(128)(2,1)} %get-tuple-element.35) | copy-start | bytes 6148
  357.6 56.9 %copy-start.146 = (bf16[1024]{0:T(1024)(128)(2,1)S(1)}, bf16[1024]{0:T(1024)(128)(2,1)}, u32[]{:S(2)}) copy-start(bf16[1024]{0:T(1024)(128)(2,1)} %get-tuple-element.36) | copy-start | bytes 6148
  357.6 57.0 %copy-start.145 = (bf16[1024]{0:T(1024)(128)(2,1)S(1)}, bf16[1024]{0:T(1024)(128)(2,1)}, u32[]{:S(2)}) copy-start(bf16[1024]{0:T(1024)(128)(2,1)} %get-tuple-element.37) | copy-start | bytes 6148
  357.6 57.0 %copy-start.144 = (bf16[1024]{0:T(1024)(128)(2,1)S(1)}, bf16[1024]{0:T(1024)(128)(2,1)}, u32[]{:S(2)}) copy-start(bf16[1024]{0:T(1024)(128)(2,1)} %get-tuple-element.38) | copy-start | bytes 6148
  357.6 57.0 %copy-start.143 = (bf16[1024]{0:T(1024)(128)(2,1)S(1)}, bf16[1024]{0:T(1024)(128)(2,1)}, u32[]{:S(2)}) copy-start(bf16[1024]{0:T(1024)(128)(2,1)} %get-tuple-element.39) | copy-start | bytes 6148
  357.6 57.0 %copy-start.142 = (bf16[1024]{0:T(1024)(128)(2,1)S(1)}, bf16[1024]{0:T(1024)(128)(2,1)}, u32[]{:S(2)}) copy-start(bf16[1024]{0:T(1024)(128)(2,1)} %get-tuple-element.40) | copy-start | bytes 6148
  357.6 57.0 %copy-start.141 = (bf16[1024]{0:T(1024)(128)(2,1)S(1)}, bf16[1024]{0:T(1024)(128)(2,1)}, u32[]{:S(2)}) copy-start(bf16[1024]{0:T(1024)(128)(2,1)} %get-tuple-element.41) | copy-start | bytes 6148
  357.6 57.0 %copy-start.140 = (bf16[1024]{0:T(1024)(128)(2,1)S(1)}, bf16[1024]{0:T(1024)(128)(2,1)}, u32[]{:S(2)}) copy-start(bf16[1024]{0:T(1024)(128)(2,1)} %get-tuple-element.42) | copy-start | bytes 6148
  357.6 57.0 %copy-start.139 = (bf16[1024]{0:T(1024)(128)(2,1)S(1)}, bf16[1024]{0:T(1024)(128)(2,1)}, u32[]{:S(2)}) copy-start(bf16[1024]{0:T(1024)(128)(2,1)} %get-tuple-element.43) | copy-start | bytes 6148
  357.8 73.5 %collective-permute-start.3 = (bf16[6,3,1024]{2,0,1:T(8,128)(2,1)S(1)}, bf16[6,3,1024]{2,0,1:T(8,128)(2,1)S(1)}, u32[]{:S(2)}, u32[]{:S(2)}) collective-permute-start(bf16[6,3,1024]{2,0,1:T(8,128)(2,1)S(1)} %slice.2737), channel_id=1, source_target_pairs={{4,0},{8,4},{12,8},{16,12},{20,16},{24,20},{28,24},{5,1},{9,5},{13... | collective-permute-start | bytes 110600 | tf_op jit(solution)/shard_map/ppermute | solution.py:10
  431.2 100.1 %reduce-scatter.3.cloned.1.call-start = ((), (), s32[]{:S(2)}) async-start(), calls=%async_computation.5 | async-start | bytes 2621440 | tf_op jit(solution)/shard_map/reduce_scatter | solution.py:130
  449.0 244.1 %reduce-scatter.5.cloned.1.call-start = ((), (), s32[]{:S(2)}) async-start(), calls=%async_computation.6 | async-start | bytes 28311552 | tf_op jit(solution)/shard_map/reduce_scatter | solution.py:133
  (130 other events, 1997.0 us)
Sparse Core Ops, SparseCore 0:
  37.3 45.2 all-gather.2
  84.5 125.3 all-gather.4
  431.4 53.8 all-reduce.1
  488.1 43.2 reduce-scatter.2
  535.4 157.6 reduce-scatter.4
where the time goes:
time: 712 us; the launch traced here: 700 us
  waiting for transfers between devices  363 us (51%)
  other arithmetic  137 us (19%)
  local copies, waits for them, and re-layouts  77.5 us (11%)
  blocking collectives  51.9 us (7%)
  matrix products  40.4 us (6%)
  between operations  17.5 us (2%)
  starting transfers between devices  12 us (2%)
    reduce_scatter x1, waiting for transfers between devices, on_device(): lax.psum_scatter(jnp.einsum('td,tsc->dsc', tokens, grad_mixed, preferred_...  162 us
    all_gather x1, waiting for transfers between devices, on_device(): gathered = lax.all_gather(w_in, 'ctx', axis=0, tiled=True)  127 us
    another operation x130, local copies, waits for them, and re-layouts, tap_sums(): return jnp.stack(pieces, 0)  70.2 us
    reduce_sum x17, other arithmetic, tap_sums(): pieces.append(jnp.sum(grads * ext[first:first + count] * keep_mask, axis=0))  52.3 us
    another operation x4, other arithmetic, on_device(): jnp.stack([first_grad, grad_product * filtered[:, 2], grad_product * filt...  47.6 us
    all_gather x1, waiting for transfers between devices, on_device(): tokens = lax.all_gather(own_part, 'fsdp', axis=1, tiled=True)  32.9 us
    all_to_all x1, blocking collectives, on_device(): lax.all_to_all(loaded, 'ctx', split_axis=1, concat_axis=0, tiled=True)  28.4 us
    psum x1, blocking collectives, on_device(): lax.psum(jnp.transpose(short_local, (1, 0, 2)).astype(jnp.bfloat16), 'ctx')  23.5 us
  transfers between devices with their start and end apart: 9, of which 7 were waited for; matrix products, arithmetic and copies ran while one was open for 28% of the time, Pallas kernels for 0%

commit v1 on v0

v1 whole, which is shorter than its diff:
```python
import jax
import jax.numpy as jnp
from jax import lax
from jax.experimental import pallas as pl
from jax.experimental.pallas import tpu as pltpu
from jax.sharding import PartitionSpec as P

LANES = 128


def round_up(x, to):
    return -(-x // to) * to


def neighbour_rows(x, axis, by):
    size = lax.axis_size(axis)
    pairs = [(i, i + by) for i in range(size) if 0 <= i + by < size]
    return lax.ppermute(x, axis, pairs)


def rotated(x, axis, by):
    size = lax.axis_size(axis)
    return lax.ppermute(x, axis, [(i, (i + by) % size) for i in range(size)])


def gather_by_permutes(x, axis, dim):
    size = lax.axis_size(axis)
    me = lax.axis_index(axis)
    width = x.shape[dim]
    shape = list(x.shape)
    shape[dim] = width * size
    out = lax.dynamic_update_slice_in_dim(jnp.zeros(shape, x.dtype), x, me * width, dim)
    for by in range(1, size):
        got = rotated(x, axis, by)
        out = lax.dynamic_update_slice_in_dim(out, got, ((me - by) % size) * width, dim)
    return out


def swap_by_permutes(x, axis, split_dim):
    size = lax.axis_size(axis)
    me = lax.axis_index(axis)
    width = x.shape[split_dim] // size
    pieces = [(me, lax.dynamic_slice_in_dim(x, me * width, width, split_dim))]
    for by in range(1, size):
        part = lax.dynamic_slice_in_dim(x, ((me + by) % size) * width, width, split_dim)
        pieces.append(((me - by) % size, rotated(part, axis, by)))
    return pieces


def summed_over(x, axis):
    size = lax.axis_size(axis)
    if size & (size - 1):
        return lax.psum(x.astype(jnp.bfloat16), axis).astype(jnp.float32)
    step = 1
    while step < size:
        mine = x.astype(jnp.bfloat16)
        got = lax.ppermute(mine, axis, [(i, i ^ step) for i in range(size)])
        x = mine.astype(jnp.float32) + got.astype(jnp.float32)
        step *= 2
    return x


def conv_kernel(
    dims, proj, prev12, prev0, next0, next12, grads, next_grads, dist, room, short, long,
    gated, mixed, long_sums, short_sums,
    s0, s1, s2, go, f0, f1, f2, prod, back, gf, acc,
):
    rows, lead, short_pad, short_w, long_w, tail = dims
    f32 = jnp.float32
    s0[0:short_pad, :] = prev0[...].astype(f32)
    s0[short_pad : short_pad + rows, :] = proj[0].astype(f32)
    s0[short_pad + rows :, :] = next0[...].astype(f32)
    for k, ref in ((0, s1), (1, s2)):
        ref[0 : lead + short_pad, :] = prev12[k].astype(f32)
        ref[lead + short_pad : lead + short_pad + rows, :] = proj[1 + k].astype(f32)
        ref[lead + short_pad + rows :, :] = next12[k].astype(f32)
    go[0:rows, :] = grads[...].astype(f32)
    go[rows:, :] = next_grads[...].astype(f32)

    def rounded(x):
        return x.astype(jnp.bfloat16).astype(f32)

    step = 8 * 7 if (lead + rows + tail) % 56 == 0 else 8

    def lead_short(ref, taps, base, reach, n):
        total = jnp.zeros((n, LANES), f32)
        for j in range(short_w):
            x = ref[pl.ds(base + short_pad - j, n), :]
            total = total + jnp.where(reach >= j, x, 0.0) * taps[j : j + 1, :]
        return total

    def before(i, _):
        base = pl.multiple_of(i * step, 8)
        reach = dist[pl.ds(base, step), :]
        a = lead_short(s1, short[1], base, reach, step)
        b = lead_short(s2, short[2], base, reach, step)
        f1[pl.ds(base, step), :] = a
        f2[pl.ds(base, step), :] = b
        prod[pl.ds(base, step), :] = rounded(a * b)
        return 0

    lax.fori_loop(0, (lead + rows + tail) // step, before, 0)

    def after(i, _):
        base = pl.multiple_of(i * step, 8)
        reach = dist[pl.ds(base + lead, step), :]
        a = lead_short(s0, short[0], base, reach, step)
        f0[pl.ds(base, step), :] = a
        back[pl.ds(base, step), :] = rounded(go[pl.ds(base, step), :] * a)
        return 0

    lax.fori_loop(0, (rows + tail + lead) // step, after, 0)

    acc[...] = jnp.zeros_like(acc)
    unroll = 8

    def long_tile(base, n, own):
        reach = dist[pl.ds(base + lead, n), :]
        ahead = room[pl.ds(base, n), :]
        here = back[pl.ds(base, n), :]

        def taps_step(i, carry):
            carried, grad = carry
            for u in range(unroll):
                j = i * unroll + u
                tap = long[pl.ds(j, 1), :]
                x = jnp.where(reach >= j, prod[pl.ds(base + lead - j, n), :], 0.0)
                y = jnp.where(ahead >= j, back[pl.ds(base + j, n), :], 0.0)
                carried = carried + x * tap
                grad = grad + y * tap
                if own:
                    z = here * x
                    part = z[0:8, :]
                    for r in range(8, n, 8):
                        part = part + z[r : r + 8, :]
                    at = pl.multiple_of(j * 8, 8)
                    acc[pl.ds(at, 8), :] += part
            return carried, grad

        zero = jnp.zeros((n, LANES), f32)
        carried, grad = lax.fori_loop(0, long_w // unroll, taps_step, (zero, zero))
        if own:
            gated[pl.ds(base, n), :] = (f0[pl.ds(base, n), :] * carried).astype(gated.dtype)
        gf[0, pl.ds(base, n), :] = rounded(go[pl.ds(base, n), :] * carried)
        gf[1, pl.ds(base, n), :] = rounded(grad * f2[pl.ds(base + lead, n), :])
        gf[2, pl.ds(base, n), :] = rounded(grad * f1[pl.ds(base + lead, n), :])

    tile = 64 if rows % 64 == 0 else 8
    lax.fori_loop(
        0, rows // tile, lambda i, _: (long_tile(pl.multiple_of(i * tile, 8), tile, True), 0)[1], 0
    )
    for extra in range(0, tail, 8):
        long_tile(rows + extra, 8, False)
    long_sums[...] = jnp.sum(acc[...].reshape(long_w, 8, LANES), axis=1)

    short_sums[...] = jnp.zeros_like(short_sums)

    def last(i, _):
        base = pl.multiple_of(i * tile, 8)
        reach = dist[pl.ds(base + lead, tile), :]
        ahead = room[pl.ds(base, tile), :]
        for s, ref, off in ((0, s0, 0), (1, s1, lead), (2, s2, lead)):
            total = jnp.zeros((tile, LANES), f32)
            here = gf[s, pl.ds(base, tile), :]
            for j in range(short_w):
                y = jnp.where(ahead >= j, gf[s, pl.ds(base + j, tile), :], 0.0)
                total = total + y * short[s, j : j + 1, :]
                x = jnp.where(reach >= j, ref[pl.ds(base + off + short_pad - j, tile), :], 0.0)
                short_sums[s, j : j + 1, :] += jnp.sum(here * x, axis=0, keepdims=True)
            mixed[s, pl.ds(base, tile), :] = total.astype(mixed.dtype)
        return 0

    lax.fori_loop(0, rows // tile, last, 0)


def conv_block(proj, grad_out, short_taps, long_taps, contig_lengths):
    _, rows, chans = proj.shape
    short_w, long_w = short_taps.shape[1], long_taps.shape[0]
    short_pad = 16
    lead = round_up(long_w, 16)
    tail = round_up(short_w - 1, 8)
    far = lead + short_pad

    up = neighbour_rows(proj[1:, rows - far :], "ctx", 1)
    up0 = neighbour_rows(proj[0, rows - short_pad :], "ctx", 1)
    down0 = neighbour_rows(proj[0, :far], "ctx", -1)
    down12 = neighbour_rows(proj[1:, :short_pad], "ctx", -1)
    down_grads = neighbour_rows(grad_out[:far], "ctx", -1)

    offset = lax.axis_index("ctx") * rows
    ends = jnp.cumsum(contig_lengths, dtype=jnp.int32)
    begins = ends - contig_lengths
    at = offset - lead + jnp.arange(lead + rows + far, dtype=jnp.int32)
    first = jnp.max(jnp.where(begins[None, :] <= at[:, None], begins[None, :], 0), axis=1)
    dist = jnp.broadcast_to((at - first)[:, None], (at.shape[0], LANES))
    here = offset + jnp.arange(rows + short_pad, dtype=jnp.int32)
    big = jnp.int32(2**30)
    end = jnp.min(jnp.where(ends[None, :] > here[:, None], ends[None, :], big), axis=1)
    room = jnp.broadcast_to((end - 1 - here)[:, None], (here.shape[0], LANES))

    def block(*lead_dims):
        n = len(lead_dims)
        return pl.BlockSpec((*lead_dims, LANES), lambda i: (0,) * n + (i,))

    def whole(r):
        return pl.BlockSpec((r, LANES), lambda i: (0, 0))

    def vmem(*shape):
        return pltpu.VMEM((*shape, LANES), jnp.float32)

    span = lead + rows + tail
    dims = (rows, lead, short_pad, short_w, long_w, tail)
    return pl.pallas_call(
        lambda *refs: conv_kernel(dims, *refs),
        grid=(chans // LANES,),
        in_specs=[
            block(3, rows), block(2, far), block(short_pad), block(far), block(2, short_pad),
            block(rows), block(far), whole(dist.shape[0]), whole(room.shape[0]),
            block(3, short_w), block(long_w),
        ],
        out_specs=[block(rows), block(3, rows), block(long_w), block(3, 8 * -(-short_w // 8))],
        out_shape=[
            jax.ShapeDtypeStruct((rows, chans), jnp.bfloat16),
            jax.ShapeDtypeStruct((3, rows, chans), jnp.bfloat16),
            jax.ShapeDtypeStruct((long_w, chans), jnp.float32),
            jax.ShapeDtypeStruct((3, 8 * -(-short_w // 8), chans), jnp.float32),
        ],
        scratch_shapes=[
            vmem(short_pad + rows + far), vmem(far + rows + short_pad),
            vmem(far + rows + short_pad), vmem(rows + far),
            vmem(span), vmem(span), vmem(span), vmem(span), vmem(span),
            vmem(3, rows + short_pad), vmem(long_w * 8),
        ],
        compiler_params=pltpu.CompilerParams(vmem_limit_bytes=40 << 20),
        cost_estimate=pl.CostEstimate(
            flops=rows * chans * long_w * 10, bytes_accessed=rows * chans * 24, transcendentals=0
        ),
        name="hyena_filters",
    )(proj, up, up0, down0, down12, grad_out, down_grads, dist, room, short_taps, long_taps)


def on_device(loaded, slot_pos, contig_lengths, w_in, short_taps, long_taps, grad_out):
    f32, bf16 = jnp.float32, jnp.bfloat16
    rows, chans = grad_out.shape
    short_w, long_w = short_taps.shape[1], long_taps.shape[0]
    weights = lax.all_gather(jnp.transpose(w_in, (1, 0, 2)), "ctx", axis=1, tiled=True)

    moved = lax.all_to_all(loaded, "ctx", split_axis=1, concat_axis=0, tiled=True)
    slot_rows = moved.reshape(-1, moved.shape[3])
    targets = slot_pos.reshape(-1)
    picker = (targets[None, :] == jnp.arange(rows, dtype=jnp.int32)[:, None]).astype(bf16)
    own_part = jnp.dot(picker, slot_rows, preferred_element_type=f32).astype(bf16)
    tokens = gather_by_permutes(own_part, "fsdp", 1)

    proj = jnp.einsum("td,sdc->stc", tokens, weights, preferred_element_type=f32).astype(bf16)
    later_tokens, proj = lax.optimization_barrier((tokens, proj))
    gated_out, mixed, long_local, short_local = conv_block(
        proj, grad_out, short_taps, long_taps, contig_lengths
    )

    n_ctx = lax.axis_size("ctx")
    feats = tokens.shape[1] // n_ctx
    all_tokens = jnp.zeros((n_ctx * rows, feats), bf16)
    for source, piece in swap_by_permutes(later_tokens, "ctx", 1):
        all_tokens = lax.dynamic_update_slice_in_dim(all_tokens, piece, source * rows, 0)

    all_mixed = lax.all_gather(mixed, "ctx", axis=1, tiled=True)

    partial = jnp.einsum("stc,sdc->td", mixed, weights, preferred_element_type=f32).astype(bf16)
    token_grads = sum(
        piece.astype(f32) for _, piece in swap_by_permutes(partial, "fsdp", 1)
    ).astype(bf16)

    filter_grads = summed_over(
        jnp.concatenate([long_local, short_local.reshape(-1, chans)], 0), "ctx"
    )
    long_total = filter_grads[:long_w]
    short_total = filter_grads[long_w:].reshape(3, -1, chans)[:, :short_w]

    weight_grads = jnp.einsum(
        "td,stc->sdc", all_tokens, all_mixed, preferred_element_type=f32
    ).astype(bf16)
    return (
        gated_out, token_grads, jnp.transpose(weight_grads, (1, 0, 2)), short_total, long_total,
    )


def solution(mesh):
    in_specs = (
        P("ctx", None, None, "fsdp"),
        P("ctx", None, None),
        P(),
        P("ctx", None, "fsdp"),
        P(None, None, "fsdp"),
        P(None, "fsdp"),
        P("ctx", "fsdp"),
    )
    out_specs = (
        P("ctx", "fsdp"),
        P("ctx", "fsdp"),
        P("ctx", None, "fsdp"),
        P(None, None, "fsdp"),
        P(None, "fsdp"),
    )
    return jax.shard_map(
        on_device, mesh=mesh, in_specs=in_specs, out_specs=out_specs, check_vma=False
    )
```

time: 712 us -> 383 us (0.54); the launches traced: 700 us -> 380 us
  waiting for transfers between devices: 363 us -> 174 us
  other arithmetic: 137 us -> 2.85 us
  Pallas kernels: 0 us -> 75.2 us
  local copies, waits for them, and re-layouts: 77.5 us -> 19.8 us
  blocking collectives: 51.9 us -> 0 us
  starting transfers between devices: 12 us -> 55.9 us
    reduce_scatter x2 -> x0, waiting for transfers between devices: 176 us -> none  [the longest x1 162 us: on_device(): lax.psum_scatter(jnp.einsum('td,tsc->dsc', tokens, grad_mixed, preferred_...]
    all_gather x2, waiting for transfers between devices: 160 us -> 50 us  [the longest x1 50 us: on_device(): lax.all_gather(jnp.transpose(w_in, (1, 0, 2)), 'ctx', axis=1, tiled=True)]
    ppermute x4 -> x21, waiting for transfers between devices: 3.95 us -> 91.2 us  [the longest x13 85.6 us: rotated(): return lax.ppermute(x, axis, [(i, (i + by) % size) for i in range(size)])]
    pallas_call x0 -> x1, Pallas kernels: none -> 75.2 us  [conv_block(): pl.pallas_call(lambda *refs: conv_kernel(dims, *refs), grid=(chans // LAN...]
    another operation x131 -> x1, local copies, waits for them, and re-layouts: 70.3 us -> 0.08 us  [the longest x130 70.2 us: tap_sums(): return jnp.stack(pieces, 0)]
    reduce_sum x17 -> x0, other arithmetic: 52.3 us -> none  [tap_sums(): pieces.append(jnp.sum(grads * ext[first:first + count] * keep_mask, axis=0))]
    another operation x6 -> x3, other arithmetic: 47.8 us -> 0.19 us  [the longest x4 47.6 us: on_device(): jnp.stack([first_grad, grad_product * filtered[:, 2], grad_product * filt...]
    ppermute x4 -> x21, starting transfers between devices: 11.8 us -> 51.2 us  [the longest x13 21.6 us: rotated(): return lax.ppermute(x, axis, [(i, (i + by) % size) for i in range(size)])]
  transfers between devices with their start and end apart: 9 -> 24, of which waited for: 7 -> 12; matrix products, arithmetic and copies ran while one was open for 28% -> 13% of each run, Pallas kernels for 0% -> 0%
where the time goes in v1:
time: 383 us; the launch traced here: 380 us
  waiting for transfers between devices  174 us (45%)
  Pallas kernels  75.2 us (20%)
  starting transfers between devices  55.9 us (15%)
  matrix products  37.1 us (10%)
  local copies, waits for them, and re-layouts  19.8 us (5%)
  between operations  14.6 us (4%)
    ppermute x13, waiting for transfers between devices, rotated(): return lax.ppermute(x, axis, [(i, (i + by) % size) for i in range(size)])  85.6 us
    pallas_call x1, Pallas kernels, conv_block(): pl.pallas_call(lambda *refs: conv_kernel(dims, *refs), grid=(chans // LAN...  75.2 us
    all_gather x1, waiting for transfers between devices, on_device(): lax.all_gather(jnp.transpose(w_in, (1, 0, 2)), 'ctx', axis=1, tiled=True)  50 us
    all_to_all x1, waiting for transfers between devices, on_device(): lax.all_to_all(loaded, 'ctx', split_axis=1, concat_axis=0, tiled=True)  32.3 us
    ppermute x13, starting transfers between devices, rotated(): return lax.ppermute(x, axis, [(i, (i + by) % size) for i in range(size)])  21.6 us
    ppermute x3, starting transfers between devices, summed_over(): got = lax.ppermute(mine, axis, [(i, i ^ step) for i in range(size)])  17.6 us
    dot_general x1, matrix products, on_device(): jnp.einsum('stc,sdc->td', mixed, weights, preferred_element_type=f32)  13 us
    ppermute x5, starting transfers between devices, neighbour_rows(): return lax.ppermute(x, axis, pairs)  12 us
  transfers between devices with their start and end apart: 24, of which 12 were waited for; matrix products, arithmetic and copies ran while one was open for 13% of the time, Pallas kernels for 0%

profile of v1, /device:TPU:15, one launch (start us, length us, event | category | flops | bytes accessed | tf_op | source)
XLA Modules:
  0.0 379.7 jit_solution(5069534310890866281)
XLA Ops:
  7.2 0.7 all-gather.3.cloned.1.call-update
  7.9 4.7 %all-to-all-start = ((bf16[1,8,128,1024]{3,2,0,1:T(8,128)(2,1)}), bf16[1,8,128,1024]{3,2,0,1:T(8,128)(2,1)S(1)}, u32[]{:S(2)}, u32[]{:S(2)}) async-start(bf16[1,8,128,1024]{3,2,0,1:T(8,128)(2,1)} %bitcast.1), calls=%async_computation | async-start | bytes 4194304 | tf_op jit(solution)/shard_map/all_to_all | solution.py:248
  12.6 0.7 slice.28
  13.3 2.3 collective-permute-start.7
  15.7 0.1 copy.37
  15.8 0.1 reduce
  16.0 0.1 select_reduce_fusion.1
  16.0 32.3 %all-to-all-done = bf16[1,8,128,1024]{3,2,0,1:T(8,128)(2,1)S(1)} async-done(((bf16[1,8,128,1024]{3,2,0,1:T(8,128)(2,1)}), bf16[1,8,128,1024]{3,2,0,1:T(8,128)(2,1)S(1)}, u32[]{:S(2)}, u32[]{:S(2)}) %all-to-all-start) | async-done | bytes 2097184 | tf_op jit(solution)/shard_map/all_to_all | solution.py:248
  48.3 1.5 convolution_convert_fusion.1
  49.8 1.4 collective-permute-start
  51.2 1.1 collective-permute-start.1
  52.3 1.5 collective-permute-start.2
  53.8 0.1 select_reduce_fusion
  53.9 1.2 copy.32
  55.2 0.1 broadcast_in_dim.24
  55.4 5.5 %collective-permute-done = bf16[256,1024]{1,0:T(8,128)(2,1)} collective-permute-done((bf16[256,1024]{1,0:T(8,128)(2,1)}, bf16[256,1024]{1,0:T(8,128)(2,1)}, u32[]{:S(2)}, u32[]{:S(2)}) %collective-permute-start) | collective-permute-done | bytes 524320 | tf_op jit(solution)/shard_map/ppermute | solution.py:23
  60.9 1.2 copy.33
  62.1 31.6 %collective-permute-done.1 = bf16[256,1024]{1,0:T(8,128)(2,1)} collective-permute-done((bf16[256,1024]{1,0:T(8,128)(2,1)}, bf16[256,1024]{1,0:T(8,128)(2,1)}, u32[]{:S(2)}, u32[]{:S(2)}) %collective-permute-start.1) | collective-permute-done | bytes 524320 | tf_op jit(solution)/shard_map/ppermute | solution.py:23
  93.7 2.0 copy.34
  95.8 3.0 collective-permute-done.2
  98.8 2.2 copy.35
  101.0 1.1 constant_dynamic-update-slice_fusion.8
  102.2 50.0 %all-gather.3.cloned.1.call-done = bf16[3,4096,1024]{2,1,0:T(8,128)(2,1)} async-done(((bf16[3,512,1024]{2,1,0:T(8,128)(2,1)}), bf16[3,4096,1024]{2,1,0:T(8,128)(2,1)}) %all-gather.3.cloned.1.call-update) | async-done | bytes 25165840 | tf_op jit(solution)/shard_map/all_gather | solution.py:246
  152.3 11.8 %fusion.7.refs_0_ = bf16[3,256,1024]{2,1,0:T(8,128)(2,1)S(1)} fusion(bf16[3,4096,1024]{2,1,0:T(8,128)(2,1)} %all-gather.3.cloned.1.call-done, bf16[256,4096]{0,1:T(8,128)(2,1)S(1)} %constant_dynamic-update-slice_fusion.7), kind=kOutput, calls=%fused_computation.7 | convolution fusion | flops 6443237376 | bytes 28835840 | tf_op jit(solution)/shard_map/td,sdc->stc/dot_general | solution.py:255
  164.2 1.4 collective-permute-start.3
  165.6 3.0 collective-permute-start.5
  168.7 1.3 collective-permute-start.4
  170.0 4.0 %collective-permute-start.6 = (bf16[2,16,1024]{2,1,0:T(8,128)(2,1)S(1)}, bf16[2,16,1024]{2,1,0:T(8,128)(2,1)S(1)}, u32[]{:S(2)}, u32[]{:S(2)}) collective-permute-start(bf16[2,16,1024]{2,1,0:T(8,128)(2,1)S(1)} %slice.27), channel_id=1, source_target_pairs={{4,0},{8,4},{12,8},{16,12},{20,16},{24,20},{28,24},{5,1},{9,5},{13... | collective-permute-start | bytes 196616 | tf_op jit(solution)/shard_map/ppermute | solution.py:18
  174.1 0.8 collective-permute-done.6.refs_4_
  174.9 0.1 broadcast_in_dim.30.refs_7_
  175.1 0.1 broadcast_in_dim.32.refs_8_
  175.2 75.2 %hyena_filters.1 = (bf16[256,1024]{1,0:T(8,128)(2,1)}, bf16[3,256,1024]{2,1,0:T(8,128)(2,1)}, f32[128,1024]{1,0:T(8,128)S(1)}, f32[3,8,1024]{2,1,0:T(8,128)S(1)}) custom-call(bf16[3,256,1024]{2,1,0:T(8,128)(2,1)S(1)} %fusion.7.refs_0_, bf16[2,144,1024]{2,1,0:T(8,128)(2,1)S(1)} %collective-permute-done.3.refs_1_, ...), custom_call_target="tpu_custom_call" | custom-call | flops 335544320 | bytes 6291456 | tf_op jit(solution)/shard_map/hyena_filters/pallas_call | solution.py:213
  250.5 0.2 broadcast_in_dim.50
  250.8 1.1 constant_dynamic-slice_fusion
  251.8 1.3 copy-done.3
  253.1 2.5 collective-permute-start.11
  255.6 3.0 collective-permute-start.12
  258.7 1.1 collective-permute-start.13
  259.8 1.0 collective-permute-start.14
  260.8 1.0 collective-permute-start.15
  261.8 2.7 collective-permute-start.16
  264.5 0.7 constant_dynamic-update-slice_fusion.6
  265.2 10.0 %collective-permute-done.12 = bf16[256,512]{0,1:T(8,128)(2,1)S(1)} collective-permute-done((bf16[256,512]{0,1:T(8,128)(2,1)}, bf16[256,512]{0,1:T(8,128)(2,1)S(1)}, u32[]{:S(2)}, u32[]{:S(2)}) %collective-permute-start.12) | collective-permute-done | bytes 262176 | tf_op jit(solution)/shard_map/ppermute | solution.py:23
  275.2 0.8 constant_dynamic-update-slice_fusion.5
  276.0 1.4 collective-permute-done.13
  277.4 0.8 constant_dynamic-update-slice_fusion.4
  278.2 0.8 constant_dynamic-update-slice_fusion.3
  279.1 1.0 collective-permute-start.18
  280.0 13.0 %fusion = bf16[256,4096]{1,0:T(8,128)(2,1)} fusion(bf16[3,256,1024]{2,1,0:T(8,128)(2,1)} %get-tuple-element.13, bf16[3,4096,1024]{2,1,0:T(8,128)(2,1)} %all-gather.3.cloned.1.call-done), kind=kOutput, calls=%fused_computation.1 | convolution fusion | flops 6443499520 | bytes 28835840 | tf_op jit(solution)/shard_map/stc,sdc->td/dot_general | solution.py:269
  293.1 16.6 %collective-permute-start.19 = (bf16[152,1024]{1,0:T(8,128)(2,1)S(1)}, bf16[152,1024]{1,0:T(8,128)(2,1)S(1)}, u32[]{:S(2)}, u32[]{:S(2)}) collective-permute-start(bf16[152,1024]{1,0:T(8,128)(2,1)S(1)} %add_convert_fusion.2), channel_id=1, source_target_pairs={{0,8},{4,12},{8,0},{12,4},{16,24},{20,28},{24,16},{28,20},{1,9},{5... | collective-permute-start | bytes 933896 | tf_op jit(solution)/shard_map/ppermute | solution.py:57
  309.7 1.5 constant_dynamic-slice_fusion.9
  311.3 2.4 collective-permute-start.9
  313.7 2.1 collective-permute-start.8
  315.8 1.0 constant_dynamic-update-slice_fusion.2
  316.8 1.7 collective-permute-start.17
  318.5 1.0 constant_dynamic-update-slice_fusion.1
  319.5 4.7 %collective-permute-done.19 = bf16[152,1024]{1,0:T(8,128)(2,1)S(1)} collective-permute-done((bf16[152,1024]{1,0:T(8,128)(2,1)S(1)}, bf16[152,1024]{1,0:T(8,128)(2,1)S(1)}, u32[]{:S(2)}, u32[]{:S(2)}) %collective-permute-start.19) | collective-permute-done | bytes 311328 | tf_op jit(solution)/shard_map/ppermute | solution.py:57
  324.3 7.7 %collective-permute-done.17 = bf16[256,512]{0,1:T(8,128)(2,1)S(1)} collective-permute-done((bf16[256,512]{0,1:T(8,128)(2,1)S(1)}, bf16[256,512]{0,1:T(8,128)(2,1)S(1)}, u32[]{:S(2)}, u32[]{:S(2)}) %collective-permute-start.17) | collective-permute-done | bytes 262176 | tf_op jit(solution)/shard_map/ppermute | solution.py:23
  332.1 15.1 %collective-permute-done.9 = bf16[256,1024]{1,0:T(8,128)(2,1)S(1)} collective-permute-done((bf16[256,1024]{1,0:T(8,128)(2,1)S(1)}, bf16[256,1024]{1,0:T(8,128)(2,1)S(1)}, u32[]{:S(2)}, u32[]{:S(2)}) %collective-permute-start.9) | collective-permute-done | bytes 524320 | tf_op jit(solution)/shard_map/ppermute | solution.py:23
  347.1 11.2 %collective-permute-done.8 = bf16[256,1024]{1,0:T(8,128)(2,1)S(1)} collective-permute-done((bf16[256,1024]{1,0:T(8,128)(2,1)S(1)}, bf16[256,1024]{1,0:T(8,128)(2,1)S(1)}, u32[]{:S(2)}, u32[]{:S(2)}) %collective-permute-start.8) | collective-permute-done | bytes 524320 | tf_op jit(solution)/shard_map/ppermute | solution.py:23
  358.4 2.2 add_convert_fusion
  360.6 0.8 slice.34
  361.5 0.6 slice_bitcast_fusion.1
  362.1 10.8 %convolution_convert_fusion = bf16[512,3,1024]{2,0,1:T(8,128)(2,1)} fusion(bf16[3,2048,1024]{2,1,0:T(8,128)(2,1)} %all-gather.5.cloned.1.call-done, bf16[2048,512]{0,1:T(8,128)(2,1)S(1)} %constant_dynamic-update-slice_fusion), kind=kOutput, calls=%fused_computation.2 | convolution fusion | flops 6444023808 | bytes 17825792 | tf_op jit(solution)/shard_map/td,stc->sdc/dot_general | solution.py:280
  (52 shorter events, 0.8 us)
Async XLA Ops:
  7.2 145.1 %all-gather.3.cloned.1.call-start = ((), (), s32[]{:S(2)}) async-start(), calls=%async_computation.1 | async-start | bytes 28311552 | tf_op jit(solution)/shard_map/all_gather | solution.py:246
  7.9 4.7 %copy-start = (bf16[256,1024]{1,0:T(8,128)(2,1)S(1)}, bf16[256,1024]{1,0:T(8,128)(2,1)}, u32[]{:S(2)}) copy-start(bf16[256,1024]{1,0:T(8,128)(2,1)} %refs_5_.1) | copy-start | bytes 1572868
  7.9 7.8 %copy-start.6 = (s32[16]{0:T(128)S(1)}, s32[16]{0:T(128)}, u32[]{:S(2)}) copy-start(s32[16]{0:T(128)} %param.9) | copy-start | bytes 196
  7.9 40.4 %copy-start.7 = (s32[1,8,128]{2,1,0:T(8,128)S(1)}, s32[1,8,128]{2,1,0:T(8,128)}, u32[]{:S(2)}) copy-start(s32[1,8,128]{2,1,0:T(8,128)} %param.8) | copy-start | bytes 12292
  7.9 40.4 %all-to-all-start = ((bf16[1,8,128,1024]{3,2,0,1:T(8,128)(2,1)}), bf16[1,8,128,1024]{3,2,0,1:T(8,128)(2,1)S(1)}, u32[]{:S(2)}, u32[]{:S(2)}) async-start(bf16[1,8,128,1024]{3,2,0,1:T(8,128)(2,1)} %bitcast.1), calls=%async_computation | async-start | bytes 4194304 | tf_op jit(solution)/shard_map/all_to_all | solution.py:248
  12.6 349.5 %all-gather.5.cloned.1.call-start = ((), (), s32[]{:S(2)}) async-start(), calls=%async_computation.2 | async-start | bytes 14155776 | tf_op jit(solution)/shard_map/all_gather | solution.py:267
  13.3 160.7 %collective-permute-start.7 = (bf16[144,1024]{1,0:T(8,128)(2,1)}, bf16[144,1024]{1,0:T(8,128)(2,1)S(1)}, u32[]{:S(2)}, u32[]{:S(2)}) collective-permute-start(bf16[144,1024]{1,0:T(8,128)(2,1)} %slice.28), channel_id=1, source_target_pairs={{4,0},{8,4},{12,8},{16,12},{20,16},{24,20},{28,24},{5,1},{9,5},{13... | collective-permute-start | bytes 884744 | tf_op jit(solution)/shard_map/ppermute | solution.py:18
  49.8 11.0 %collective-permute-start = (bf16[256,1024]{1,0:T(8,128)(2,1)}, bf16[256,1024]{1,0:T(8,128)(2,1)}, u32[]{:S(2)}, u32[]{:S(2)}) collective-permute-start(bf16[256,1024]{1,0:T(8,128)(2,1)} %convolution_convert_fusion.1), channel_id=1, source_target_pairs={{0,1},{1,2},{2,3},{3,0},{4,5},{5,6},{6,7},{7,4},{8,9},{9,10},{10,1... | collective-permute-start | bytes 1572872 | tf_op jit(solution)/shard_map/ppermute | solution.py:23
  51.2 42.5 %collective-permute-start.1 = (bf16[256,1024]{1,0:T(8,128)(2,1)}, bf16[256,1024]{1,0:T(8,128)(2,1)}, u32[]{:S(2)}, u32[]{:S(2)}) collective-permute-start(bf16[256,1024]{1,0:T(8,128)(2,1)} %convolution_convert_fusion.1), channel_id=1, source_target_pairs={{0,2},{1,3},{2,0},{3,1},{4,6},{5,7},{6,4},{7,5},{8,10},{9,11},{10,... | collective-permute-start | bytes 1572872 | tf_op jit(solution)/shard_map/ppermute | solution.py:23
  52.3 46.4 %collective-permute-start.2 = (bf16[256,1024]{1,0:T(8,128)(2,1)}, bf16[256,1024]{1,0:T(8,128)(2,1)}, u32[]{:S(2)}, u32[]{:S(2)}) collective-permute-start(bf16[256,1024]{1,0:T(8,128)(2,1)} %convolution_convert_fusion.1), channel_id=1, source_target_pairs={{0,3},{1,0},{2,1},{3,2},{4,7},{5,4},{6,5},{7,6},{8,11},{9,8},{10,9... | collective-permute-start | bytes 1572872 | tf_op jit(solution)/shard_map/ppermute | solution.py:23
  101.0 1.2 copy-start.5
  164.1 11.1 %copy-start.1 = (f32[128,1024]{1,0:T(8,128)S(1)}, f32[128,1024]{1,0:T(8,128)}, u32[]{:S(2)}) copy-start(f32[128,1024]{1,0:T(8,128)} %refs_10_.1) | copy-start | bytes 1572868
  164.1 11.1 %copy-start.2 = (f32[3,7,1024]{2,1,0:T(8,128)S(1)}, f32[3,7,1024]{2,1,0:T(8,128)}, u32[]{:S(2)}) copy-start(f32[3,7,1024]{2,1,0:T(8,128)} %refs_9_.1) | copy-start | bytes 258052
  164.2 10.7 %collective-permute-start.3 = (bf16[2,144,1024]{2,1,0:T(8,128)(2,1)S(1)}, bf16[2,144,1024]{2,1,0:T(8,128)(2,1)S(1)}, u32[]{:S(2)}, u32[]{:S(2)}) collective-permute-start(bf16[2,144,1024]{2,1,0:T(8,128)(2,1)S(1)} %slice.24), channel_id=1, source_target_pairs={{0,4},{4,8},{8,12},{12,16},{16,20},{20,24},{24,28},{1,5},{5,9},{9,... | collective-permute-start | bytes 1769480 | tf_op jit(solution)/shard_map/ppermute | solution.py:18
  165.6 9.3 %collective-permute-start.5 = (bf16[144,1024]{1,0:T(8,128)(2,1)S(1)}, bf16[144,1024]{1,0:T(8,128)(2,1)S(1)}, u32[]{:S(2)}, u32[]{:S(2)}) collective-permute-start(bf16[144,1024]{1,0:T(8,128)(2,1)S(1)} %slice_bitcast_fusion), channel_id=1, source_target_pairs={{4,0},{8,4},{12,8},{16,12},{20,16},{24,20},{28,24},{5,1},{9,5},{13... | collective-permute-start | bytes 884744 | tf_op jit(solution)/shard_map/ppermute | solution.py:18
  168.7 5.3 %collective-permute-start.4 = (bf16[16,1024]{1,0:T(8,128)(2,1)S(1)}, bf16[16,1024]{1,0:T(8,128)(2,1)S(1)}, u32[]{:S(2)}, u32[]{:S(2)}) collective-permute-start(bf16[16,1024]{1,0:T(8,128)(2,1)S(1)} %slice_bitcast_fusion.2), channel_id=1, source_target_pairs={{0,4},{4,8},{8,12},{12,16},{16,20},{20,24},{24,28},{1,5},{5,9},{9,... | collective-permute-start | bytes 98312 | tf_op jit(solution)/shard_map/ppermute | solution.py:18
  170.0 4.9 %collective-permute-start.6 = (bf16[2,16,1024]{2,1,0:T(8,128)(2,1)S(1)}, bf16[2,16,1024]{2,1,0:T(8,128)(2,1)S(1)}, u32[]{:S(2)}, u32[]{:S(2)}) collective-permute-start(bf16[2,16,1024]{2,1,0:T(8,128)(2,1)S(1)} %slice.27), channel_id=1, source_target_pairs={{4,0},{8,4},{12,8},{16,12},{20,16},{24,20},{28,24},{5,1},{9,5},{13... | collective-permute-start | bytes 196616 | tf_op jit(solution)/shard_map/ppermute | solution.py:18
  251.8 1.3 copy-start.3
  253.1 8.7 %collective-permute-start.11 = (bf16[256,512]{0,1:T(8,128)(2,1)}, bf16[256,512]{0,1:T(8,128)(2,1)S(1)}, u32[]{:S(2)}, u32[]{:S(2)}) collective-permute-start(bf16[256,512]{0,1:T(8,128)(2,1)} %get-tuple-element.23), channel_id=1, source_target_pairs={{0,4},{4,8},{8,12},{12,16},{16,20},{20,24},{24,28},{28,0},{1,5},{5... | collective-permute-start | bytes 786440 | tf_op jit(solution)/shard_map/ppermute | solution.py:23
  255.6 19.6 %collective-permute-start.12 = (bf16[256,512]{0,1:T(8,128)(2,1)}, bf16[256,512]{0,1:T(8,128)(2,1)S(1)}, u32[]{:S(2)}, u32[]{:S(2)}) collective-permute-start(bf16[256,512]{0,1:T(8,128)(2,1)} %get-tuple-element.22), channel_id=1, source_target_pairs={{0,8},{4,12},{8,16},{12,20},{16,24},{20,28},{24,0},{28,4},{1,9},{5... | collective-permute-start | bytes 786440 | tf_op jit(solution)/shard_map/ppermute | solution.py:23
  258.7 18.8 %collective-permute-start.13 = (bf16[256,512]{0,1:T(8,128)(2,1)S(1)}, bf16[256,512]{0,1:T(8,128)(2,1)S(1)}, u32[]{:S(2)}, u32[]{:S(2)}) collective-permute-start(bf16[256,512]{0,1:T(8,128)(2,1)S(1)} %get-tuple-element.21), channel_id=1, source_target_pairs={{0,12},{4,16},{8,20},{12,24},{16,28},{20,0},{24,4},{28,8},{1,13},{... | collective-permute-start | bytes 786440 | tf_op jit(solution)/shard_map/ppermute | solution.py:23
  259.8 18.5 %collective-permute-start.14 = (bf16[256,512]{0,1:T(8,128)(2,1)S(1)}, bf16[256,512]{0,1:T(8,128)(2,1)S(1)}, u32[]{:S(2)}, u32[]{:S(2)}) collective-permute-start(bf16[256,512]{0,1:T(8,128)(2,1)S(1)} %get-tuple-element.20), channel_id=1, source_target_pairs={{0,16},{4,20},{8,24},{12,28},{16,0},{20,4},{24,8},{28,12},{1,17},{... | collective-permute-start | bytes 786440 | tf_op jit(solution)/shard_map/ppermute | solution.py:23
  260.8 52.9 %collective-permute-start.15 = (bf16[256,512]{0,1:T(8,128)(2,1)}, bf16[256,512]{0,1:T(8,128)(2,1)}, u32[]{:S(2)}, u32[]{:S(2)}) collective-permute-start(bf16[256,512]{0,1:T(8,128)(2,1)} %get-tuple-element.19), channel_id=1, source_target_pairs={{0,20},{4,24},{8,28},{12,0},{16,4},{20,8},{24,12},{28,16},{1,21},{... | collective-permute-start | bytes 786440 | tf_op jit(solution)/shard_map/ppermute | solution.py:23
  261.8 55.0 %collective-permute-start.16 = (bf16[256,512]{0,1:T(8,128)(2,1)}, bf16[256,512]{0,1:T(8,128)(2,1)}, u32[]{:S(2)}, u32[]{:S(2)}) collective-permute-start(bf16[256,512]{0,1:T(8,128)(2,1)} %get-tuple-element.18), channel_id=1, source_target_pairs={{0,24},{4,28},{8,0},{12,4},{16,8},{20,12},{24,16},{28,20},{1,25},{... | collective-permute-start | bytes 786440 | tf_op jit(solution)/shard_map/ppermute | solution.py:23
  279.1 14.0 %collective-permute-start.18 = (bf16[152,1024]{1,0:T(8,128)(2,1)S(1)}, bf16[152,1024]{1,0:T(8,128)(2,1)S(1)}, u32[]{:S(2)}, u32[]{:S(2)}) collective-permute-start(bf16[152,1024]{1,0:T(8,128)(2,1)S(1)} %pad_maximum_fusion), channel_id=1, source_target_pairs={{0,4},{4,0},{8,12},{12,8},{16,20},{20,16},{24,28},{28,24},{1,5},{5... | collective-permute-start | bytes 933896 | tf_op jit(solution)/shard_map/ppermute | solution.py:57
  293.1 22.7 %copy-start.4 = (bf16[2048,512]{0,1:T(8,128)(2,1)S(1)}, bf16[2048,512]{0,1:T(8,128)(2,1)}, u32[]{:S(2)}) copy-start(bf16[2048,512]{0,1:T(8,128)(2,1)} %constant_dynamic-update-slice_fusion.3) | copy-start | bytes 6291460
  293.1 31.0 %collective-permute-start.19 = (bf16[152,1024]{1,0:T(8,128)(2,1)S(1)}, bf16[152,1024]{1,0:T(8,128)(2,1)S(1)}, u32[]{:S(2)}, u32[]{:S(2)}) collective-permute-start(bf16[152,1024]{1,0:T(8,128)(2,1)S(1)} %add_convert_fusion.2), channel_id=1, source_target_pairs={{0,8},{4,12},{8,0},{12,4},{16,24},{20,28},{24,16},{28,20},{1,9},{5... | collective-permute-start | bytes 933896 | tf_op jit(solution)/shard_map/ppermute | solution.py:57
  311.2 20.8 %collective-permute-start.10 = (bf16[256,1024]{1,0:T(8,128)(2,1)S(1)}, bf16[256,1024]{1,0:T(8,128)(2,1)S(1)}, u32[]{:S(2)}, u32[]{:S(2)}) collective-permute-start(bf16[256,1024]{1,0:T(8,128)(2,1)S(1)} %get-tuple-element.26), channel_id=1, source_target_pairs={{0,3},{1,0},{2,1},{3,2},{4,7},{5,4},{6,5},{7,6},{8,11},{9,8},{10,9... | collective-permute-start | bytes 1572872 | tf_op jit(solution)/shard_map/ppermute | solution.py:23
  311.3 35.8 %collective-permute-start.9 = (bf16[256,1024]{1,0:T(8,128)(2,1)S(1)}, bf16[256,1024]{1,0:T(8,128)(2,1)S(1)}, u32[]{:S(2)}, u32[]{:S(2)}) collective-permute-start(bf16[256,1024]{1,0:T(8,128)(2,1)S(1)} %get-tuple-element.27), channel_id=1, source_target_pairs={{0,2},{1,3},{2,0},{3,1},{4,6},{5,7},{6,4},{7,5},{8,10},{9,11},{10,... | collective-permute-start | bytes 1572872 | tf_op jit(solution)/shard_map/ppermute | solution.py:23
  313.7 44.7 %collective-permute-start.8 = (bf16[256,1024]{1,0:T(8,128)(2,1)S(1)}, bf16[256,1024]{1,0:T(8,128)(2,1)S(1)}, u32[]{:S(2)}, u32[]{:S(2)}) collective-permute-start(bf16[256,1024]{1,0:T(8,128)(2,1)S(1)} %get-tuple-element.25), channel_id=1, source_target_pairs={{0,1},{1,2},{2,3},{3,0},{4,5},{5,6},{6,7},{7,4},{8,9},{9,10},{10,1... | collective-permute-start | bytes 1572872 | tf_op jit(solution)/shard_map/ppermute | solution.py:23
  316.8 15.2 %collective-permute-start.17 = (bf16[256,512]{0,1:T(8,128)(2,1)S(1)}, bf16[256,512]{0,1:T(8,128)(2,1)S(1)}, u32[]{:S(2)}, u32[]{:S(2)}) collective-permute-start(bf16[256,512]{0,1:T(8,128)(2,1)S(1)} %get-tuple-element.17), channel_id=1, source_target_pairs={{0,28},{4,0},{8,4},{12,8},{16,12},{20,16},{24,20},{28,24},{1,29},{... | collective-permute-start | bytes 786440 | tf_op jit(solution)/shard_map/ppermute | solution.py:23
  324.3 36.3 %collective-permute-start.20 = (bf16[152,1024]{1,0:T(8,128)(2,1)S(1)}, bf16[152,1024]{1,0:T(8,128)(2,1)S(1)}, u32[]{:S(2)}, u32[]{:S(2)}) collective-permute-start(bf16[152,1024]{1,0:T(8,128)(2,1)S(1)} %add_convert_fusion.1), channel_id=1, source_target_pairs={{0,16},{4,20},{8,24},{12,28},{16,0},{20,4},{24,8},{28,12},{1,17},{... | collective-permute-start | bytes 933896 | tf_op jit(solution)/shard_map/ppermute | solution.py:57
Sparse Core Ops, SparseCore 0:
  9.9 142.3 all-gather.2
  250.5 102.9 all-gather.4

commit v2 on v1

--- a/solution.py
+++ b/solution.py
@@ -239,11 +239,46 @@
     )(proj, up, up0, down0, down12, grad_out, down_grads, dist, room, short_taps, long_taps)
 
 
+def weight_kernel(tokens_t, grads, *rest):
+    rest[-1][...] = jnp.dot(
+        tokens_t[...], grads[...], preferred_element_type=jnp.float32
+    ).astype(jnp.bfloat16)
+
+
+def weight_part(tokens_t, grads, before, part, chans):
+    feats, count = tokens_t.shape
+    streams, _, width = grads.shape
+    more = () if before is None else (before,)
+    return pl.pallas_call(
+        weight_kernel,
+        grid=(streams,),
+        in_specs=[
+            pl.BlockSpec((feats, count), lambda s: (0, 0)),
+            pl.BlockSpec((None, count, width), lambda s: (s, 0, 0)),
+        ] + [pl.BlockSpec(memory_space=pl.ANY) for _ in more],
+        out_specs=pl.BlockSpec((None, feats, width), lambda s: (s, 0, part)),
+        out_shape=jax.ShapeDtypeStruct((streams, feats, chans), jnp.bfloat16),
+        input_output_aliases={2: 0} if more else {},
+        compiler_params=pltpu.CompilerParams(vmem_limit_bytes=58 << 20),
+        cost_estimate=pl.CostEstimate(
+            flops=2 * feats * count * streams * width,
+            bytes_accessed=2 * streams * width * (count + feats) + 2 * feats * count,
+            transcendentals=0,
+        ),
+        name="weight_grads",
+    )(tokens_t, grads, *more)
+
+
 def on_device(loaded, slot_pos, contig_lengths, w_in, short_taps, long_taps, grad_out):
     f32, bf16 = jnp.float32, jnp.bfloat16
     rows, chans = grad_out.shape
     short_w, long_w = short_taps.shape[1], long_taps.shape[0]
-    weights = lax.all_gather(jnp.transpose(w_in, (1, 0, 2)), "ctx", axis=1, tiled=True)
+    parts = 2 if chans % (2 * LANES) == 0 else 1
+    width = chans // parts
+    cuts = [slice(p * width, (p + 1) * width) for p in range(parts)]
+
+    by_stream = jnp.transpose(w_in, (1, 0, 2))
+    weights = [lax.all_gather(by_stream[:, :, c], "ctx", axis=1, tiled=True) for c in cuts]
 
     moved = lax.all_to_all(loaded, "ctx", split_axis=1, concat_axis=0, tiled=True)
     slot_rows = moved.reshape(-1, moved.shape[3])
@@ -252,36 +287,44 @@
     own_part = jnp.dot(picker, slot_rows, preferred_element_type=f32).astype(bf16)
     tokens = gather_by_permutes(own_part, "fsdp", 1)
 
-    proj = jnp.einsum("td,sdc->stc", tokens, weights, preferred_element_type=f32).astype(bf16)
-    later_tokens, proj = lax.optimization_barrier((tokens, proj))
-    gated_out, mixed, long_local, short_local = conv_block(
-        proj, grad_out, short_taps, long_taps, contig_lengths
-    )
-
-    n_ctx = lax.axis_size("ctx")
-    feats = tokens.shape[1] // n_ctx
-    all_tokens = jnp.zeros((n_ctx * rows, feats), bf16)
-    for source, piece in swap_by_permutes(later_tokens, "ctx", 1):
-        all_tokens = lax.dynamic_update_slice_in_dim(all_tokens, piece, source * rows, 0)
-
-    all_mixed = lax.all_gather(mixed, "ctx", axis=1, tiled=True)
-
-    partial = jnp.einsum("stc,sdc->td", mixed, weights, preferred_element_type=f32).astype(bf16)
+    gated, mixed, gathered, sums = [], [], [], []
+    partial = None
+    pieces = swap_by_permutes(tokens, "ctx", 1)
+    sources = [source for source, _ in pieces]
+    pieces = [piece for _, piece in pieces]
+    for p, c in enumerate(cuts):
+        held = weights[p]
+        if p:
+            held, mixed[-1], partial = lax.optimization_barrier((held, mixed[-1], partial))
+        proj = jnp.einsum("td,sdc->stc", tokens, held, preferred_element_type=f32).astype(bf16)
+        out, grads, long_local, short_local = conv_block(
+            proj, grad_out[:, c], short_taps[:, :, c], long_taps[:, c], contig_lengths
+        )
+        if p == 0:
+            grads, *pieces = lax.optimization_barrier((grads, *pieces))
+        gated.append(out)
+        mixed.append(grads)
+        sums.append(jnp.concatenate([long_local, short_local.reshape(-1, width)], 0))
+        gathered.append(lax.all_gather(grads, "ctx", axis=1, tiled=True))
+        term = jnp.einsum("stc,sdc->td", grads, held, preferred_element_type=f32)
+        partial = term if partial is None else partial + term
     token_grads = sum(
-        piece.astype(f32) for _, piece in swap_by_permutes(partial, "fsdp", 1)
+        piece.astype(f32) for _, piece in swap_by_permutes(partial.astype(bf16), "fsdp", 1)
     ).astype(bf16)
 
-    filter_grads = summed_over(
-        jnp.concatenate([long_local, short_local.reshape(-1, chans)], 0), "ctx"
-    )
+    filter_grads = summed_over(jnp.concatenate(sums, 1), "ctx")
     long_total = filter_grads[:long_w]
     short_total = filter_grads[long_w:].reshape(3, -1, chans)[:, :short_w]
 
-    weight_grads = jnp.einsum(
-        "td,stc->sdc", all_tokens, all_mixed, preferred_element_type=f32
-    ).astype(bf16)
+    n_ctx = lax.axis_size("ctx")
+    tokens_t = jnp.zeros((tokens.shape[1] // n_ctx, n_ctx * rows), bf16)
+    for source, piece in zip(sources, pieces):
+        tokens_t = lax.dynamic_update_slice_in_dim(tokens_t, piece.T, source * rows, 1)
+    weight_grads = None
+    for p, g in enumerate(gathered):
+        weight_grads = weight_part(tokens_t, g, weight_grads, p, chans)
     return (
-        gated_out, token_grads, jnp.transpose(weight_grads, (1, 0, 2)), short_total, long_total,
+        jnp.concatenate(gated, 1), token_grads, jnp.transpose(weight_grads, (1, 0, 2)), short_total, long_total,
     )
 
 

time: 383 us -> 350 us (0.914)
  waiting for transfers between devices: 174 us -> 131 us
  Pallas kernels: 75.2 us -> 89.7 us
    all_gather x2 -> x4, waiting for transfers between devices: 50 us -> 3.7 us  [the longest x2 3.7 us: on_device(): lax.all_gather(by_stream[:, :, c], 'ctx', axis=1, tiled=True)]
    pallas_call x0 -> x2, Pallas kernels: none -> 14.6 us  [weight_part(): pl.pallas_call(weight_kernel, grid=(streams,), in_specs=[pl.BlockSpec((fe...]
    ppermute x5 -> x10, starting transfers between devices: 12 us -> 22.3 us  [neighbour_rows(): return lax.ppermute(x, axis, pairs)]
    ppermute x3, starting transfers between devices: 17.6 us -> 8.91 us  [summed_over(): got = lax.ppermute(mine, axis, [(i, i ^ step) for i in range(size)])]
    ppermute x3 -> x0, local copies, waits for them, and re-layouts: 5.48 us -> none  [rotated(): return lax.ppermute(x, axis, [(i, (i + by) % size) for i in range(size)])]
    ppermute x13, waiting for transfers between devices: 85.6 us -> 81.2 us  [rotated(): return lax.ppermute(x, axis, [(i, (i + by) % size) for i in range(size)])]
    all_to_all x1, waiting for transfers between devices: 32.3 us -> 36.3 us  [on_device(): lax.all_to_all(loaded, 'ctx', split_axis=1, concat_axis=0, tiled=True)]
    slice x0 -> x4, local copies, waits for them, and re-layouts: none -> 4.02 us  [the longest x1 3.94 us: on_device(): by_stream[:, :, c]]
  transfers between devices with their start and end apart: 24 -> 31, of which waited for: 12 -> 11; matrix products, arithmetic and copies ran while one was open for 13% -> 15% of each run, Pallas kernels for 0% -> 24%
where the time goes in v2:
time: 350 us; the launch traced here: 349 us
  waiting for transfers between devices  131 us (37%)
  Pallas kernels  89.7 us (26%)
  starting transfers between devices  54.9 us (16%)
  matrix products  39.6 us (11%)
  local copies, waits for them, and re-layouts  16.7 us (5%)
  between operations  14.5 us (4%)
    ppermute x13, waiting for transfers between devices, rotated(): return lax.ppermute(x, axis, [(i, (i + by) % size) for i in range(size)])  81.2 us
    pallas_call x2, Pallas kernels, conv_block(): pl.pallas_call(lambda *refs: conv_kernel(dims, *refs), grid=(chans // LAN...  75.1 us
    all_to_all x1, waiting for transfers between devices, on_device(): lax.all_to_all(loaded, 'ctx', split_axis=1, concat_axis=0, tiled=True)  36.3 us
    ppermute x10, starting transfers between devices, neighbour_rows(): return lax.ppermute(x, axis, pairs)  22.3 us
    dot_general x2, matrix products, on_device(): term = jnp.einsum('stc,sdc->td', grads, held, preferred_element_type=f32)  19.9 us
    ppermute x13, starting transfers between devices, rotated(): return lax.ppermute(x, axis, [(i, (i + by) % size) for i in range(size)])  18.9 us
    dot_general x2, matrix products, on_device(): jnp.einsum('td,sdc->stc', tokens, held, preferred_element_type=f32)  17.8 us
    pallas_call x2, Pallas kernels, weight_part(): pl.pallas_call(weight_kernel, grid=(streams,), in_specs=[pl.BlockSpec((fe...  14.6 us
  transfers between devices with their start and end apart: 31, of which 11 were waited for; matrix products, arithmetic and copies ran while one was open for 15% of the time, Pallas kernels for 24%

profile of v2, /device:TPU:15, one launch (start us, length us, event | category | flops | bytes accessed | tf_op | source)
XLA Modules:
  0.0 349.5 jit_solution(6529530284101307949)
XLA Ops:
  7.2 3.9 %fusion.20 = (bf16[3,512,512]{2,1,0:T(8,128)(2,1)}, bf16[3,512,512]{2,1,0:T(8,128)(2,1)}) fusion(bf16[3,512,1024]{2,1,0:T(8,128)(2,1)} %bitcast.71), kind=kLoop, calls=%fused_computation.57 | loop fusion | bytes 6291456 | tf_op jit(solution)/shard_map/slice | solution.py:281
  11.2 0.7 all-gather.7.cloned.1.call-update
  12.0 4.7 %all-to-all-start = ((bf16[1,8,128,1024]{3,2,0,1:T(8,128)(2,1)}), bf16[1,8,128,1024]{3,2,0,1:T(8,128)(2,1)S(1)}, u32[]{:S(2)}, u32[]{:S(2)}) async-start(bf16[1,8,128,1024]{3,2,0,1:T(8,128)(2,1)} %bitcast.1), calls=%async_computation | async-start | bytes 4194304 | tf_op jit(solution)/shard_map/all_to_all | solution.py:283
  16.6 0.7 fusion.22
  17.3 2.3 collective-permute-start.7
  20.0 36.3 %all-to-all-done = bf16[1,8,128,1024]{3,2,0,1:T(8,128)(2,1)S(1)} async-done(((bf16[1,8,128,1024]{3,2,0,1:T(8,128)(2,1)}), bf16[1,8,128,1024]{3,2,0,1:T(8,128)(2,1)S(1)}, u32[]{:S(2)}, u32[]{:S(2)}) %all-to-all-start) | async-done | bytes 2097184 | tf_op jit(solution)/shard_map/all_to_all | solution.py:283
  56.3 1.5 broadcast_in_dim.36
  57.7 1.9 constant_dynamic-update-slice_fusion.3
  59.7 1.3 collective-permute-start
  60.9 1.0 collective-permute-start.1
  62.0 1.5 collective-permute-start.2
  63.5 8.1 %collective-permute-done = bf16[256,1024]{0,1:T(8,128)(2,1)S(1)} collective-permute-done((bf16[256,1024]{0,1:T(8,128)(2,1)}, bf16[256,1024]{0,1:T(8,128)(2,1)S(1)}, u32[]{:S(2)}, u32[]{:S(2)}) %collective-permute-start) | collective-permute-done | bytes 524320 | tf_op jit(solution)/shard_map/ppermute | solution.py:23
  71.6 0.8 constant_dynamic-update-slice_fusion.2
  72.4 32.0 %collective-permute-done.1 = bf16[256,1024]{0,1:T(8,128)(2,1)S(1)} collective-permute-done((bf16[256,1024]{0,1:T(8,128)(2,1)}, bf16[256,1024]{0,1:T(8,128)(2,1)S(1)}, u32[]{:S(2)}, u32[]{:S(2)}) %collective-permute-start.1) | collective-permute-done | bytes 524320 | tf_op jit(solution)/shard_map/ppermute | solution.py:23
  104.4 0.8 constant_dynamic-update-slice_fusion.1
  105.2 3.1 collective-permute-done.2
  108.3 0.8 constant_dynamic-update-slice_fusion
  109.1 2.5 constant_dynamic-slice_fusion.3
  111.6 0.7 collective-permute-start.10
  112.3 1.2 collective-permute-start.11
  113.5 9.2 %fusion.15.refs_0_ = bf16[3,256,512]{2,1,0:T(8,128)(2,1)S(1)} fusion(bf16[3,4096,512]{2,1,0:T(8,128)(2,1)} %all-gather.5.cloned.1.call-done, bf16[256,4096]{0,1:T(8,128)(2,1)} %constant_dynamic-update-slice_fusion), kind=kOutput, calls=%fused_computation.11 | convolution fusion | flops 3221618688 | bytes 15466496 | tf_op jit(solution)/shard_map/td,sdc->stc/dot_general | solution.py:299
  122.7 1.3 collective-permute-start.3
  124.0 3.0 collective-permute-start.5
  127.1 3.5 collective-permute-start.6
  130.6 1.3 collective-permute-start.4
  132.0 1.8 collective-permute-done.11
  133.8 0.4 collective-permute-start.12
  134.2 6.0 %collective-permute-start.13 = (bf16[256,512]{0,1:T(8,128)(2,1)}, bf16[256,512]{0,1:T(8,128)(2,1)S(1)}, u32[]{:S(2)}, u32[]{:S(2)}) collective-permute-start(bf16[256,512]{0,1:T(8,128)(2,1)} %get-tuple-element.49), channel_id=1, source_target_pairs={{0,24},{4,28},{8,0},{12,4},{16,8},{20,12},{24,16},{28,20},{1,25},{... | collective-permute-start | bytes 786440 | tf_op jit(solution)/shard_map/ppermute | solution.py:23
  140.2 1.0 collective-permute-start.14
  141.2 1.7 collective-permute-start.8
  142.8 0.6 collective-permute-start.9
  143.5 0.1 broadcast_in_dim.38.refs_7_
  143.8 37.6 %hyena_filters.2 = (bf16[256,512]{1,0:T(8,128)(2,1)S(1)}, bf16[3,256,512]{2,1,0:T(8,128)(2,1)}, f32[128,512]{1,0:T(8,128)S(1)}, f32[3,8,512]{2,1,0:T(8,128)S(1)}) custom-call(bf16[3,256,512]{2,1,0:T(8,128)(2,1)S(1)} %fusion.15.refs_0_, bf16[2,144,512]{2,1,0:T(8,128)(2,1)S(1)} %collective-permute-done.3.refs_1_, ...), custom_call_target="tpu_custom_call" | custom-call | flops 167772160 | bytes 3145728 | tf_op jit(solution)/shard_map/hyena_filters/pallas_call | solution.py:213
  181.4 0.6 copy-done.7
  182.3 0.7 copy-done.13
  183.1 1.9 collective-permute-start.19
  185.0 10.5 %convolution_bitcast_fusion.1 = f32[256,4096]{1,0:T(8,128)} fusion(bf16[3,256,512]{2,1,0:T(8,128)(2,1)} %get-tuple-element.26, bf16[3,4096,512]{2,1,0:T(8,128)(2,1)} %all-gather.5.cloned.1.call-done), kind=kOutput, calls=%fused_computation.1 | convolution fusion | flops 3221225472 | bytes 17563648 | tf_op jit(solution)/shard_map/stc,sdc->td/dot_general | solution.py:309
  195.4 3.7 %all-gather.7.cloned.1.call-done = bf16[3,4096,512]{2,1,0:T(8,128)(2,1)} async-done(((bf16[3,512,512]{2,1,0:T(8,128)(2,1)}), bf16[3,4096,512]{2,1,0:T(8,128)(2,1)}) %all-gather.7.cloned.1.call-update) | async-done | bytes 12582928 | tf_op jit(solution)/shard_map/all_gather | solution.py:281
  199.1 8.6 %fusion.12.refs_0_ = bf16[3,256,512]{2,1,0:T(8,128)(2,1)S(1)} fusion(bf16[3,4096,512]{2,1,0:T(8,128)(2,1)} %all-gather.7.cloned.1.call-done, bf16[256,4096]{0,1:T(8,128)(2,1)} %constant_dynamic-update-slice_fusion), kind=kOutput, calls=%fused_computation.10 | convolution fusion | flops 3221618688 | bytes 15466496 | tf_op jit(solution)/shard_map/td,sdc->stc/dot_general | solution.py:299
  207.8 1.3 collective-permute-start.15
  209.1 3.0 collective-permute-start.17
  212.2 3.4 collective-permute-start.18
  215.6 1.3 collective-permute-start.16
  216.9 1.8 collective-permute-done.16.refs_2_
  218.7 37.5 %hyena_filters.3 = (bf16[256,512]{1,0:T(8,128)(2,1)S(1)}, bf16[3,256,512]{2,1,0:T(8,128)(2,1)}, f32[128,512]{1,0:T(8,128)S(1)}, f32[3,8,512]{2,1,0:T(8,128)S(1)}) custom-call(bf16[3,256,512]{2,1,0:T(8,128)(2,1)S(1)} %fusion.12.refs_0_, bf16[2,144,512]{2,1,0:T(8,128)(2,1)S(1)} %collective-permute-done.15.refs_1_, ...), custom_call_target="tpu_custom_call" | custom-call | flops 167772160 | bytes 3145728 | tf_op jit(solution)/shard_map/hyena_filters/pallas_call | solution.py:213
  256.5 0.2 broadcast_in_dim.41
  256.8 0.4 copy-done.12
  257.4 1.0 bitcast_dynamic-update-slice_fusion.3
  258.6 5.6 %collective-permute-start.23 = (bf16[152,1024]{1,0:T(8,128)(2,1)S(1)}, bf16[152,1024]{1,0:T(8,128)(2,1)S(1)}, u32[]{:S(2)}, u32[]{:S(2)}) collective-permute-start(bf16[152,1024]{1,0:T(8,128)(2,1)S(1)} %maximum_maximum_fusion), channel_id=1, source_target_pairs={{0,4},{4,0},{8,12},{12,8},{16,20},{20,16},{24,28},{28,24},{1,5},{5... | collective-permute-start | bytes 933896 | tf_op jit(solution)/shard_map/ppermute | solution.py:57
  264.2 9.4 %fusion.1 = bf16[256,4096]{1,0:T(8,128)(2,1)S(1)} fusion(f32[256,4096]{1,0:T(8,128)} %convolution_bitcast_fusion.1, bf16[3,256,512]{2,1,0:T(8,128)(2,1)} %get-tuple-element.30, bf16[3,4096,512]{2,1,0:T(8,128)(2,1)} %all-gather.7.cloned.1.call-done), kind=kOutput, calls=%fused_computation.3 | convolution fusion | flops 3223322624 | bytes 19660800 | tf_op jit(solution)/shard_map/stc,sdc->td/dot_general | solution.py:309
  273.8 3.2 collective-permute-start.24
  277.1 1.3 collective-permute-start.20
  278.4 1.1 collective-permute-start.21
  279.5 1.3 collective-permute-start.22
  280.8 7.6 %collective-permute-done.24 = bf16[152,1024]{1,0:T(8,128)(2,1)S(1)} collective-permute-done((bf16[152,1024]{1,0:T(8,128)(2,1)S(1)}, bf16[152,1024]{1,0:T(8,128)(2,1)S(1)}, u32[]{:S(2)}, u32[]{:S(2)}) %collective-permute-start.24) | collective-permute-done | bytes 311328 | tf_op jit(solution)/shard_map/ppermute | solution.py:57
  288.5 0.9 pad_maximum_fusion
  289.4 1.1 collective-permute-done.20
  290.4 32.7 %collective-permute-done.21 = bf16[256,1024]{1,0:T(8,128)(2,1)S(1)} collective-permute-done((bf16[256,1024]{1,0:T(8,128)(2,1)S(1)}, bf16[256,1024]{1,0:T(8,128)(2,1)S(1)}, u32[]{:S(2)}, u32[]{:S(2)}) %collective-permute-start.21) | collective-permute-done | bytes 524320 | tf_op jit(solution)/shard_map/ppermute | solution.py:23
  323.2 2.5 collective-permute-done.22
  325.6 1.1 add_convert_fusion
  326.8 0.8 slice.98
  327.7 0.6 slice_bitcast_fusion.2
  328.3 7.3 %weight_grads.2.rest_0_ = bf16[3,512,1024]{2,1,0:T(8,128)(2,1)} custom-call(bf16[512,2048]{1,0:T(8,128)(2,1)} %copy-done, bf16[3,2048,512]{2,1,0:T(8,128)(2,1)} %all-gather.11.cloned.1.call-done.grads), custom_call_target="tpu_custom_call" | custom-call | flops 3221225472 | bytes 9961472 | tf_op jit(solution)/shard_map/weight_grads/pallas_call | solution.py:252
  335.6 7.3 %weight_grads.3 = bf16[3,512,1024]{2,1,0:T(8,128)(2,1)} custom-call(bf16[512,2048]{1,0:T(8,128)(2,1)} %copy-done, bf16[3,2048,512]{2,1,0:T(8,128)(2,1)} %all-gather.9.cloned.1.call-done.grads, bf16[3,512,1024]{2,1,0:T(8,128)(2,1)} %weight_grads.2.rest_0_), custom_call_target="tpu_custom_call", output_to_operand_aliasing={{}: (2, {})} | custom-call | flops 3221225472 | bytes 9961472 | tf_op jit(solution)/shard_map/weight_grads/pallas_call | solution.py:252
  (99 shorter events, 2.1 us)
Async XLA Ops:
  7.2 106.3 %all-gather.5.cloned.1.call-start = ((), (), s32[]{:S(2)}) async-start(), calls=%async_computation.1 | async-start | bytes 14155776 | tf_op jit(solution)/shard_map/all_gather | solution.py:281
  11.2 188.0 %all-gather.7.cloned.1.call-start = ((), (), s32[]{:S(2)}) async-start(), calls=%async_computation.2 | async-start | bytes 14155776 | tf_op jit(solution)/shard_map/all_gather | solution.py:281
  11.9 4.7 %copy-start.1 = (bf16[256,1024]{1,0:T(8,128)(2,1)S(1)}, bf16[256,1024]{1,0:T(8,128)(2,1)}, u32[]{:S(2)}) copy-start(bf16[256,1024]{1,0:T(8,128)(2,1)} %param.13) | copy-start | bytes 1572868
  11.9 7.6 %copy-start.16 = (s32[16]{0:T(128)S(1)}, s32[16]{0:T(128)}, u32[]{:S(2)}) copy-start(s32[16]{0:T(128)} %param.9) | copy-start | bytes 196
  12.0 8.0 %copy-start.15 = (f32[3,7,1024]{2,1,0:T(8,128)S(1)}, f32[3,7,1024]{2,1,0:T(8,128)}, u32[]{:S(2)}) copy-start(f32[3,7,1024]{2,1,0:T(8,128)} %param.11) | copy-start | bytes 258052
  12.0 44.3 %all-to-all-start = ((bf16[1,8,128,1024]{3,2,0,1:T(8,128)(2,1)}), bf16[1,8,128,1024]{3,2,0,1:T(8,128)(2,1)S(1)}, u32[]{:S(2)}, u32[]{:S(2)}) async-start(bf16[1,8,128,1024]{3,2,0,1:T(8,128)(2,1)} %bitcast.1), calls=%async_computation | async-start | bytes 4194304 | tf_op jit(solution)/shard_map/all_to_all | solution.py:283
  16.6 41.1 %copy-start.17 = (s32[1,8,128]{2,1,0:T(8,128)S(1)}, s32[1,8,128]{2,1,0:T(8,128)}, u32[]{:S(2)}) copy-start(s32[1,8,128]{2,1,0:T(8,128)} %param.8) | copy-start | bytes 12292
  16.6 311.7 %all-gather.11.cloned.1.call-start = ((), (), s32[]{:S(2)}) async-start(), calls=%async_computation.4 | async-start | bytes 7077888 | tf_op jit(solution)/shard_map/all_gather | solution.py:308
  17.3 109.8 %collective-permute-start.7 = (bf16[144,512]{1,0:T(8,128)(2,1)}, bf16[144,512]{1,0:T(8,128)(2,1)S(1)}, u32[]{:S(2)}, u32[]{:S(2)}) collective-permute-start(bf16[144,512]{1,0:T(8,128)(2,1)} %get-tuple-element.59), channel_id=1, source_target_pairs={{4,0},{8,4},{12,8},{16,12},{20,16},{24,20},{28,24},{5,1},{9,5},{13... | collective-permute-start | bytes 442376 | tf_op jit(solution)/shard_map/ppermute | solution.py:18
  59.7 11.9 %collective-permute-start = (bf16[256,1024]{0,1:T(8,128)(2,1)}, bf16[256,1024]{0,1:T(8,128)(2,1)S(1)}, u32[]{:S(2)}, u32[]{:S(2)}) collective-permute-start(bf16[256,1024]{0,1:T(8,128)(2,1)} %get-tuple-element.65), channel_id=1, source_target_pairs={{0,1},{1,2},{2,3},{3,0},{4,5},{5,6},{6,7},{7,4},{8,9},{9,10},{10,1... | collective-permute-start | bytes 1572872 | tf_op jit(solution)/shard_map/ppermute | solution.py:23
  60.9 43.4 %collective-permute-start.1 = (bf16[256,1024]{0,1:T(8,128)(2,1)}, bf16[256,1024]{0,1:T(8,128)(2,1)S(1)}, u32[]{:S(2)}, u32[]{:S(2)}) collective-permute-start(bf16[256,1024]{0,1:T(8,128)(2,1)} %get-tuple-element.65), channel_id=1, source_target_pairs={{0,2},{1,3},{2,0},{3,1},{4,6},{5,7},{6,4},{7,5},{8,10},{9,11},{10,... | collective-permute-start | bytes 1572872 | tf_op jit(solution)/shard_map/ppermute | solution.py:23
  62.0 46.3 %collective-permute-start.2 = (bf16[256,1024]{0,1:T(8,128)(2,1)}, bf16[256,1024]{0,1:T(8,128)(2,1)S(1)}, u32[]{:S(2)}, u32[]{:S(2)}) collective-permute-start(bf16[256,1024]{0,1:T(8,128)(2,1)} %get-tuple-element.65), channel_id=1, source_target_pairs={{0,3},{1,0},{2,1},{3,2},{4,7},{5,4},{6,5},{7,6},{8,11},{9,8},{10,9... | collective-permute-start | bytes 1572872 | tf_op jit(solution)/shard_map/ppermute | solution.py:23
  111.6 18.9 %collective-permute-start.10 = (bf16[256,512]{0,1:T(8,128)(2,1)S(1)}, bf16[256,512]{0,1:T(8,128)(2,1)S(1)}, u32[]{:S(2)}, u32[]{:S(2)}) collective-permute-start(bf16[256,512]{0,1:T(8,128)(2,1)S(1)} %get-tuple-element.52), channel_id=1, source_target_pairs={{0,12},{4,16},{8,20},{12,24},{16,28},{20,0},{24,4},{28,8},{1,13},{... | collective-permute-start | bytes 786440 | tf_op jit(solution)/shard_map/ppermute | solution.py:23
  112.3 31.2 %copy-start.2 = (f32[128,1024]{1,0:T(8,128)S(1)}, f32[128,1024]{1,0:T(8,128)}, u32[]{:S(2)}) copy-start(f32[128,1024]{1,0:T(8,128)} %param.12) | copy-start | bytes 1572868
  112.3 21.5 %collective-permute-start.11 = (bf16[256,512]{0,1:T(8,128)(2,1)S(1)}, bf16[256,512]{0,1:T(8,128)(2,1)}, u32[]{:S(2)}, u32[]{:S(2)}) collective-permute-start(bf16[256,512]{0,1:T(8,128)(2,1)S(1)} %get-tuple-element.51), channel_id=1, source_target_pairs={{0,16},{4,20},{8,24},{12,28},{16,0},{20,4},{24,8},{28,12},{1,17},{... | collective-permute-start | bytes 786440 | tf_op jit(solution)/shard_map/ppermute | solution.py:23
  122.7 20.1 %collective-permute-start.3 = (bf16[2,144,512]{2,1,0:T(8,128)(2,1)S(1)}, bf16[2,144,512]{2,1,0:T(8,128)(2,1)S(1)}, u32[]{:S(2)}, u32[]{:S(2)}) collective-permute-start(bf16[2,144,512]{2,1,0:T(8,128)(2,1)S(1)} %slice.87), channel_id=1, source_target_pairs={{0,4},{4,8},{8,12},{12,16},{16,20},{20,24},{24,28},{1,5},{5,9},{9,... | collective-permute-start | bytes 884744 | tf_op jit(solution)/shard_map/ppermute | solution.py:18
  124.0 17.2 %collective-permute-start.5 = (bf16[144,512]{1,0:T(8,128)(2,1)S(1)}, bf16[144,512]{1,0:T(8,128)(2,1)S(1)}, u32[]{:S(2)}, u32[]{:S(2)}) collective-permute-start(bf16[144,512]{1,0:T(8,128)(2,1)S(1)} %slice_bitcast_fusion.1), channel_id=1, source_target_pairs={{4,0},{8,4},{12,8},{16,12},{20,16},{24,20},{28,24},{5,1},{9,5},{13... | collective-permute-start | bytes 442376 | tf_op jit(solution)/shard_map/ppermute | solution.py:18
  127.1 13.1 %collective-permute-start.6 = (bf16[2,16,512]{2,1,0:T(8,128)(2,1)S(1)}, bf16[2,16,512]{2,1,0:T(8,128)(2,1)S(1)}, u32[]{:S(2)}, u32[]{:S(2)}) collective-permute-start(bf16[2,16,512]{2,1,0:T(8,128)(2,1)S(1)} %slice.90), channel_id=1, source_target_pairs={{4,0},{8,4},{12,8},{16,12},{20,16},{24,20},{28,24},{5,1},{9,5},{13... | collective-permute-start | bytes 98312 | tf_op jit(solution)/shard_map/ppermute | solution.py:18
  130.6 12.9 %copy-start.3 = (bf16[256,512]{0,1:T(8,128)(2,1)}, bf16[256,512]{0,1:T(8,128)(2,1)S(1)}, u32[]{:S(2)}) copy-start(bf16[256,512]{0,1:T(8,128)(2,1)S(1)} %collective-permute-done.10) | copy-start | bytes 786436
  130.6 3.6 %collective-permute-start.4 = (bf16[16,512]{1,0:T(8,128)(2,1)S(1)}, bf16[16,512]{1,0:T(8,128)(2,1)S(1)}, u32[]{:S(2)}, u32[]{:S(2)}) collective-permute-start(bf16[16,512]{1,0:T(8,128)(2,1)S(1)} %slice_bitcast_fusion.4), channel_id=1, source_target_pairs={{0,4},{4,8},{8,12},{12,16},{16,20},{20,24},{24,28},{1,5},{5,9},{9,... | collective-permute-start | bytes 49160 | tf_op jit(solution)/shard_map/ppermute | solution.py:18
  133.8 47.5 %collective-permute-start.12 = (bf16[256,512]{0,1:T(8,128)(2,1)}, bf16[256,512]{0,1:T(8,128)(2,1)S(1)}, u32[]{:S(2)}, u32[]{:S(2)}) collective-permute-start(bf16[256,512]{0,1:T(8,128)(2,1)} %get-tuple-element.50), channel_id=1, source_target_pairs={{0,20},{4,24},{8,28},{12,0},{16,4},{20,8},{24,12},{28,16},{1,21},{... | collective-permute-start | bytes 786440 | tf_op jit(solution)/shard_map/ppermute | solution.py:23
  134.2 47.1 %collective-permute-start.13 = (bf16[256,512]{0,1:T(8,128)(2,1)}, bf16[256,512]{0,1:T(8,128)(2,1)S(1)}, u32[]{:S(2)}, u32[]{:S(2)}) collective-permute-start(bf16[256,512]{0,1:T(8,128)(2,1)} %get-tuple-element.49), channel_id=1, source_target_pairs={{0,24},{4,28},{8,0},{12,4},{16,8},{20,12},{24,16},{28,20},{1,25},{... | collective-permute-start | bytes 786440 | tf_op jit(solution)/shard_map/ppermute | solution.py:23
  140.2 41.1 %collective-permute-start.14 = (bf16[256,512]{0,1:T(8,128)(2,1)}, bf16[256,512]{0,1:T(8,128)(2,1)S(1)}, u32[]{:S(2)}, u32[]{:S(2)}) collective-permute-start(bf16[256,512]{0,1:T(8,128)(2,1)} %get-tuple-element.48), channel_id=1, source_target_pairs={{0,28},{4,0},{8,4},{12,8},{16,12},{20,16},{24,20},{28,24},{1,29},{... | collective-permute-start | bytes 786440 | tf_op jit(solution)/shard_map/ppermute | solution.py:23
  141.2 40.2 %collective-permute-start.8 = (bf16[256,512]{0,1:T(8,128)(2,1)}, bf16[256,512]{0,1:T(8,128)(2,1)S(1)}, u32[]{:S(2)}, u32[]{:S(2)}) collective-permute-start(bf16[256,512]{0,1:T(8,128)(2,1)} %get-tuple-element.54), channel_id=1, source_target_pairs={{0,4},{4,8},{8,12},{12,16},{16,20},{20,24},{24,28},{28,0},{1,5},{5... | collective-permute-start | bytes 786440 | tf_op jit(solution)/shard_map/ppermute | solution.py:23
  142.8 38.5 %collective-permute-start.9 = (bf16[256,512]{0,1:T(8,128)(2,1)S(1)}, bf16[256,512]{0,1:T(8,128)(2,1)S(1)}, u32[]{:S(2)}, u32[]{:S(2)}) collective-permute-start(bf16[256,512]{0,1:T(8,128)(2,1)S(1)} %get-tuple-element.53), channel_id=1, source_target_pairs={{0,8},{4,12},{8,16},{12,20},{16,24},{20,28},{24,0},{28,4},{1,9},{5... | collective-permute-start | bytes 786440 | tf_op jit(solution)/shard_map/ppermute | solution.py:23
  181.3 0.7 copy-start.7
  181.3 0.8 copy-start.9
  181.3 0.8 copy-start.5
  181.4 0.9 copy-start.11
  182.3 0.7 copy-start.13
  183.0 152.6 %all-gather.9.cloned.1.call-start = ((), (), s32[]{:S(2)}) async-start(), calls=%async_computation.3 | async-start | bytes 7077888 | tf_op jit(solution)/shard_map/all_gather | solution.py:308
  183.1 33.8 %collective-permute-start.19 = (bf16[144,512]{1,0:T(8,128)(2,1)S(1)}, bf16[144,512]{1,0:T(8,128)(2,1)S(1)}, u32[]{:S(2)}, u32[]{:S(2)}) collective-permute-start(bf16[144,512]{1,0:T(8,128)(2,1)S(1)} %get-tuple-element.58), channel_id=1, source_target_pairs={{4,0},{8,4},{12,8},{16,12},{20,16},{24,20},{28,24},{5,1},{9,5},{13... | collective-permute-start | bytes 442376 | tf_op jit(solution)/shard_map/ppermute | solution.py:18
  207.8 10.9 %collective-permute-start.15 = (bf16[2,144,512]{2,1,0:T(8,128)(2,1)S(1)}, bf16[2,144,512]{2,1,0:T(8,128)(2,1)S(1)}, u32[]{:S(2)}, u32[]{:S(2)}) collective-permute-start(bf16[2,144,512]{2,1,0:T(8,128)(2,1)S(1)} %slice.92), channel_id=1, source_target_pairs={{0,4},{4,8},{8,12},{12,16},{16,20},{20,24},{24,28},{1,5},{5,9},{9,... | collective-permute-start | bytes 884744 | tf_op jit(solution)/shard_map/ppermute | solution.py:18
  209.1 9.5 %collective-permute-start.17 = (bf16[144,512]{1,0:T(8,128)(2,1)S(1)}, bf16[144,512]{1,0:T(8,128)(2,1)S(1)}, u32[]{:S(2)}, u32[]{:S(2)}) collective-permute-start(bf16[144,512]{1,0:T(8,128)(2,1)S(1)} %slice_bitcast_fusion), channel_id=1, source_target_pairs={{4,0},{8,4},{12,8},{16,12},{20,16},{24,20},{28,24},{5,1},{9,5},{13... | collective-permute-start | bytes 442376 | tf_op jit(solution)/shard_map/ppermute | solution.py:18
  212.2 6.5 %collective-permute-start.18 = (bf16[2,16,512]{2,1,0:T(8,128)(2,1)S(1)}, bf16[2,16,512]{2,1,0:T(8,128)(2,1)S(1)}, u32[]{:S(2)}, u32[]{:S(2)}) collective-permute-start(bf16[2,16,512]{2,1,0:T(8,128)(2,1)S(1)} %slice.95), channel_id=1, source_target_pairs={{4,0},{8,4},{12,8},{16,12},{20,16},{24,20},{28,24},{5,1},{9,5},{13... | collective-permute-start | bytes 98312 | tf_op jit(solution)/shard_map/ppermute | solution.py:18
  215.6 3.1 collective-permute-start.16
  256.2 0.9 copy-start.12
  256.3 1.0 copy-start.14
  256.4 1.0 copy-start.4
  256.5 1.9 copy-start.8
  256.8 1.7 copy-start.10
  258.6 15.1 %collective-permute-start.23 = (bf16[152,1024]{1,0:T(8,128)(2,1)S(1)}, bf16[152,1024]{1,0:T(8,128)(2,1)S(1)}, u32[]{:S(2)}, u32[]{:S(2)}) collective-permute-start(bf16[152,1024]{1,0:T(8,128)(2,1)S(1)} %maximum_maximum_fusion), channel_id=1, source_target_pairs={{0,4},{4,0},{8,12},{12,8},{16,20},{20,16},{24,28},{28,24},{1,5},{5... | collective-permute-start | bytes 933896 | tf_op jit(solution)/shard_map/ppermute | solution.py:57
  273.7 7.1 %copy-start.6 = (bf16[256,512]{0,1:T(8,128)(2,1)S(1)}, bf16[256,512]{0,1:T(8,128)(2,1)}, u32[]{:S(2)}) copy-start(bf16[256,512]{0,1:T(8,128)(2,1)} %copy-done.5) | copy-start | bytes 786436
  273.8 14.6 %collective-permute-start.24 = (bf16[152,1024]{1,0:T(8,128)(2,1)S(1)}, bf16[152,1024]{1,0:T(8,128)(2,1)S(1)}, u32[]{:S(2)}, u32[]{:S(2)}) collective-permute-start(bf16[152,1024]{1,0:T(8,128)(2,1)S(1)} %add_convert_fusion.2), channel_id=1, source_target_pairs={{0,8},{4,12},{8,0},{12,4},{16,24},{20,28},{24,16},{28,20},{1,9},{5... | collective-permute-start | bytes 933896 | tf_op jit(solution)/shard_map/ppermute | solution.py:57
  277.1 13.3 %collective-permute-start.20 = (bf16[256,1024]{1,0:T(8,128)(2,1)S(1)}, bf16[256,1024]{1,0:T(8,128)(2,1)S(1)}, u32[]{:S(2)}, u32[]{:S(2)}) collective-permute-start(bf16[256,1024]{1,0:T(8,128)(2,1)S(1)} %get-tuple-element.45), channel_id=1, source_target_pairs={{0,1},{1,2},{2,3},{3,0},{4,5},{5,6},{6,7},{7,4},{8,9},{9,10},{10,1... | collective-permute-start | bytes 1572872 | tf_op jit(solution)/shard_map/ppermute | solution.py:23
  278.4 44.8 %collective-permute-start.21 = (bf16[256,1024]{1,0:T(8,128)(2,1)S(1)}, bf16[256,1024]{1,0:T(8,128)(2,1)S(1)}, u32[]{:S(2)}, u32[]{:S(2)}) collective-permute-start(bf16[256,1024]{1,0:T(8,128)(2,1)S(1)} %get-tuple-element.47), channel_id=1, source_target_pairs={{0,2},{1,3},{2,0},{3,1},{4,6},{5,7},{6,4},{7,5},{8,10},{9,11},{10,... | collective-permute-start | bytes 1572872 | tf_op jit(solution)/shard_map/ppermute | solution.py:23
  279.5 46.1 %collective-permute-start.22 = (bf16[256,1024]{1,0:T(8,128)(2,1)S(1)}, bf16[256,1024]{1,0:T(8,128)(2,1)S(1)}, u32[]{:S(2)}, u32[]{:S(2)}) collective-permute-start(bf16[256,1024]{1,0:T(8,128)(2,1)S(1)} %get-tuple-element.46), channel_id=1, source_target_pairs={{0,3},{1,0},{2,1},{3,2},{4,7},{5,4},{6,5},{7,6},{8,11},{9,8},{10,9... | collective-permute-start | bytes 1572872 | tf_op jit(solution)/shard_map/ppermute | solution.py:23
  280.8 46.0 %copy-start = (bf16[512,2048]{1,0:T(8,128)(2,1)}, bf16[512,2048]{1,0:T(8,128)(2,1)S(1)}, u32[]{:S(2)}) copy-start(bf16[512,2048]{1,0:T(8,128)(2,1)S(1)} %bitcast_dynamic-update-slice_fusion.tokens_t) | copy-start | bytes 6291460
  288.4 38.3 %collective-permute-start.25 = (bf16[152,1024]{1,0:T(8,128)(2,1)S(1)}, bf16[152,1024]{1,0:T(8,128)(2,1)S(1)}, u32[]{:S(2)}, u32[]{:S(2)}) collective-permute-start(bf16[152,1024]{1,0:T(8,128)(2,1)S(1)} %add_convert_fusion.1), channel_id=1, source_target_pairs={{0,16},{4,20},{8,24},{12,28},{16,0},{20,4},{24,8},{28,12},{1,17},{... | collective-permute-start | bytes 933896 | tf_op jit(solution)/shard_map/ppermute | solution.py:57
Sparse Core Ops, SparseCore 0:
  11.3 90.2 all-gather.4
  103.5 95.5 all-gather.6
  201.1 50.9 all-gather.10
  256.4 60.3 all-gather.8
